TPU v7x, 32 devices: a whole 2x2x4 slice. The times are simulated.
32 devices in a mesh: obs: 2 (over x), chan: 8 (over z, y), tm: 2 (over core).
Axes of the slice: x: 2, y: 2, z: 4, core: 2. Of those that a mesh axis runs over, the one named last changes fastest.
Arguments:
- residuals: bfloat16 [16, 4, 2, 1024, 1024], P(('obs', 'chan'), 'tm'), parts along dimension 0, may hold values from -0.125 to 0.125
- flag_masks: int32 [16, 4, 512], P(('obs', 'chan')), parts along dimension 0, may hold values 0 or 1
- cluster: int32 [128], P('obs'), parts along dimension 0, may hold values from 0 to 7
- penalty: float32 [16], P('obs'), parts along dimension 0, may hold values from 0.25 to 4
- jones_init: float32 [16, 1024, 256], P(('obs', 'chan')), parts along dimension 0, may hold values from -6 to 6
- duals_init: float32 [16, 1024, 256], P(('obs', 'chan')), parts along dimension 0, may hold values from -4 to 4
Outputs:
- jones_out: float32 [16, 1024, 256], P(('obs', 'chan'), 'tm'), parts along dimension 0
- duals_out: float32 [16, 1024, 256], P(('obs', 'chan'), 'tm'), parts along dimension 0
There are 2 independent parts, one for each index of `obs`. A program takes and returns all parts, laid end to end along the dimension named above; each array names one. Nothing has to cross between parts.
All inputs are finite; a program needn't handle non-finite values. No bound on the sum of `flag_masks` on one device may be relied on, other than what follows from the above.
Results may differ from a plain program's by a relative error of at most 0.0054.
Values may be sent and summed in bfloat16 or wider, within the bound.
No kernel may reach another device: no remote copies, remote signals or barrier semaphores. Data moves between devices by JAX's collectives and lax.ppermute only.
A program may use at most 64 MiB of HBM per device.

v0:
```python
import functools

import jax
import jax.numpy as jnp
import numpy as np
from jax import lax
from jax.experimental import pallas as pl
from jax.experimental.pallas import tpu as pltpu
from jax.sharding import PartitionSpec as P


POLY = 3
WIRE = jnp.bfloat16
F32 = jnp.float32
LANES = 128
TILE = 8
MIB = 1 << 20


def poly_basis(total_count):
    position = (2.0 * np.arange(total_count) + 1.0) / total_count - 1.0
    powers = np.stack([position**degree for degree in range(POLY)], axis=1)
    columns = []
    for degree in range(POLY):
        column = np.eye(POLY)[degree]
        for previous in columns:
            column = column - np.sum((powers @ column) * (powers @ previous)) * previous
        columns.append(column / np.sqrt(np.sum((powers @ column) ** 2)))
    return columns


def basis_at(channel, total_count):
    position = (2.0 * channel.astype(F32) + 1.0) * (1.0 / total_count) - 1.0
    values = []
    for column in poly_basis(total_count):
        value = jnp.float32(column[POLY - 1])
        for coefficient in column[POLY - 2 :: -1]:
            value = value * position + np.float32(coefficient)
        values.append(value)
    return values


def eye_mask(rows):
    shape = (rows, max(rows, LANES))
    return lax.broadcasted_iota(jnp.int32, shape, 0) == lax.broadcasted_iota(jnp.int32, shape, 1)


def twice(half):
    return jnp.concatenate([half, half], axis=1)


def fill_operands(xs_ref, slot, rounded, mask):
    half = rounded.shape[1] // 2
    masked = mask.astype(jnp.bfloat16) * rounded
    xs_ref[2 * slot] = masked
    xs_ref[2 * slot + 1] = jnp.concatenate([-masked[:, half:], masked[:, :half]], axis=1)


def gradient_rows(resid_ref, xs_ref, mask_ref, rows):
    total = None
    for t in range(resid_ref.shape[0]):
        product = jnp.dot(resid_ref[t, 0, rows, :], xs_ref[2 * t], preferred_element_type=F32)
        product += jnp.dot(resid_ref[t, 1, rows, :], xs_ref[2 * t + 1], preferred_element_type=F32)
        part = twice(mask_ref[t, rows, :]) * product
        total = part if total is None else total + part
    return total


def half_start(index, rows):
    return pl.multiple_of(index * rows, rows)


def first_kernel(
    resid_hbm, flags_hbm, cluster_hbm, penalty_hbm, jones_hbm, duals_hbm,
    resid_ref, grad_ref, sent_ref, mask_ref, counts_ref, inverse_ref, rates_ref, duals_ref,
    flags_ref, cluster_ref, penalty_ref, jones_ref, xs_ref, sems,
):
    rows, cols = jones_ref.shape
    _, stations = flags_ref.shape
    share, own_rows = resid_ref.shape[0], duals_ref.shape[0]
    step = rows // PIECES
    cuts = [(sum(PARTS[:m]) * step, PARTS[m] * step) for m in range(len(PARTS))]
    own = pl.ds(half_start(lax.axis_index("tm"), own_rows), own_rows)
    small = [(flags_hbm, flags_ref), (cluster_hbm, cluster_ref), (penalty_hbm, penalty_ref)]
    pieces = small + [(jones_hbm, jones_ref), (duals_hbm.at[own, :], duals_ref)]
    for start, size in cuts:
        cut = pl.ds(start, size)
        pieces.append((resid_hbm.at[:, :, cut, :], resid_ref.at[:, :, cut, :]))
    copies = [pltpu.make_async_copy(src, dst, sems.at[k]) for k, (src, dst) in enumerate(pieces)]
    streams = copies[5:]
    for copy in copies[:4] + streams[:1] + copies[4:5] + streams[1:]:
        copy.start()

    for copy in copies[:3]:
        copy.wait()
    flags = flags_ref[...].astype(F32)
    pick = (
        lax.broadcasted_iota(jnp.int32, (rows, stations), 0) // 2
        == lax.broadcasted_iota(jnp.int32, (rows, stations), 1)
    ).astype(jnp.bfloat16)

    def rows_of(line):
        spread = jnp.broadcast_to(line, (LANES, stations)).astype(jnp.bfloat16)
        return lax.dot_general(pick, spread, (((1,), (1,)), ((), ())), preferred_element_type=F32)

    for t in range(share):
        line = flags_ref[pl.ds(lax.axis_index("tm") * share + t, 1), :].astype(F32)
        mask_ref[t] = rows_of(line)
    counts_ref[...] = rows_of(jnp.sum(flags, axis=0, keepdims=True))
    dirs = cluster_ref.shape[1]
    lane = lax.broadcasted_iota(jnp.int32, (dirs, cols), 1)
    spread = lax.rem(lane, cols // 2) // 2 == lax.broadcasted_iota(jnp.int32, (dirs, cols), 0)
    labels = jnp.broadcast_to(cluster_ref[...].astype(F32), (8, dirs)).astype(jnp.bfloat16)
    label = jnp.dot(labels, spread.astype(jnp.bfloat16), preferred_element_type=F32)
    rates = jnp.zeros((8, cols), F32)
    for k in range(penalty_ref.shape[1]):
        rates = jnp.where(label == k, penalty_ref[0:1, k : k + 1], rates)
    rates_ref[...] = rates
    inverse_ref[...] = 1.0 / (twice(counts_ref[...]) + rates[0:1])

    copies[3].wait()
    rounded = jones_ref[...].astype(jnp.bfloat16)
    for t in range(share):
        fill_operands(xs_ref, t, rounded, twice(mask_ref[t]))
    for m, (start, size) in enumerate(cuts):
        cut = pl.ds(start, size)
        streams[m].wait()
        total = gradient_rows(resid_ref, xs_ref, mask_ref, cut)
        if m == 0:
            copies[4].wait()
        half, offset = divmod(start, own_rows)
        mine = rates[0:1] * (lax.axis_index("tm") == half).astype(F32)
        total = total + mine * (jones_ref[cut, :] - duals_ref[offset : offset + size])
        grad_ref[cut, :] = total
        sent_ref[cut, :] = total.astype(WIRE)


def other_kernel(
    chunks, resid_ref, mine_ref, theirs_ref, mask_ref, inverse_ref, duals_ref,
    u_ref, other_ref, xs_ref,
):
    own_rows = u_ref.shape[0]
    jones = (mine_ref[...] + theirs_ref[...].astype(F32)) * inverse_ref[...]
    rounded = jones.astype(jnp.bfloat16)
    for t in range(resid_ref.shape[0]):
        fill_operands(xs_ref, t, rounded, twice(mask_ref[t]))
    own = pl.ds(half_start(lax.axis_index("tm"), own_rows), own_rows)
    u_ref[...] = (
        mine_ref[own, :] + theirs_ref[own, :].astype(F32)
    ) * inverse_ref[own, :] + duals_ref[...]
    step = own_rows // chunks
    for m in range(chunks):
        start = half_start(1 - lax.axis_index("tm"), own_rows) + m * step
        other_ref[m * step : (m + 1) * step] = gradient_rows(
            resid_ref, xs_ref, mask_ref, pl.ds(pl.multiple_of(start, step), step)
        )


def own_kernel(
    chunks, members, resid_ref, xs_ref, mask_ref, u_ref, counts_ref, own_ref, *message_refs
):
    own_rows = own_ref.shape[0]
    step = own_rows // chunks
    base = half_start(lax.axis_index("tm"), own_rows)
    for m in range(chunks):
        own_ref[m * step : (m + 1) * step] = gradient_rows(
            resid_ref, xs_ref, mask_ref, pl.ds(pl.multiple_of(base + m * step, step), step)
        )
    block = own_rows // members
    eye = eye_mask(block)
    for s, message in enumerate(message_refs):
        offset = half_start(lax.axis_index("chan") ^ s, block)
        message[0:block] = u_ref[pl.ds(offset, block), :].astype(WIRE)
        counts = counts_ref[pl.ds(pl.multiple_of(base + offset, block), block), :]
        line = jnp.sum(jnp.where(eye, counts, 0.0), axis=0, keepdims=True)
        message[2 * block : 2 * block + TILE, 0:LANES] = jnp.broadcast_to(line, (TILE, LANES)).astype(WIRE)


def pack_kernel(members, own_ref, theirs_ref, u_ref, inverse_ref, rates_ref, *refs):
    q_ref, message_refs = refs[members], refs[members + 1 :]
    own_rows = u_ref.shape[0]
    base = half_start(lax.axis_index("tm"), own_rows)
    block = own_rows // members
    rates = rates_ref[0:1]
    for s, message in enumerate(message_refs):
        offset = half_start(lax.axis_index("chan") ^ s, block)
        rows = pl.ds(offset, block)
        u = u_ref[rows, :]
        inverse = inverse_ref[pl.ds(pl.multiple_of(base + offset, block), block), :]
        q = (own_ref[rows, :] + theirs_ref[rows, :] - rates * u) * inverse
        q_ref[rows, :] = q
        message[block : 2 * block] = (u + q).astype(WIRE)


def owner_kernel(members, block, slots, rates_ref, *refs):
    received, returned = refs[:members], refs[members:]
    rates = rates_ref[0:1]
    eye = eye_mask(block)
    table = [2.0 * rates / (float(count) + rates) for count in range(slots + 1)]
    weights = [basis_at(lax.axis_index("chan") ^ s, members) for s in range(members)]
    coeffs = [None] * POLY
    sums = [None] * POLY
    plus = lambda a, b: b if a is None else a + b
    for s in range(members):
        u = received[s][0:block].astype(F32)
        w = received[s][block : 2 * block].astype(F32)
        for p in range(POLY):
            coeffs[p] = plus(coeffs[p], weights[s][p] * u)
            sums[p] = plus(sums[p], weights[s][p] * w)
    for s in range(members):
        line = received[s][2 * block : 2 * block + TILE, 0:LANES].astype(F32)[0:1]
        counts = jnp.sum(jnp.where(eye, line, 0.0), axis=1, keepdims=True)
        first = weights[s][0] * coeffs[0]
        for p in range(1, POLY):
            first = first + weights[s][p] * coeffs[p]
        returned[s][0:block] = first.astype(WIRE)
        weight = table[0]
        for count in range(1, slots + 1):
            weight = jnp.where(counts == count, table[count], weight)
        step = weight * first
        for p in range(POLY):
            sums[p] = sums[p] + weights[s][p] * step
    for s in range(members):
        second = weights[s][0] * sums[0]
        for p in range(1, POLY):
            second = second + weights[s][p] * sums[p]
        returned[s][block : 2 * block] = second.astype(WIRE)


def finish_kernel(members, group, q_ref, u_ref, inverse_ref, rates_ref, *refs):
    received = refs[: len(group)]
    jones_hbm, duals_hbm, jones_ref, duals_ref, sems = refs[-5:]
    rates = 2.0 * rates_ref[0:1]
    own_rows = u_ref.shape[0]
    block = own_rows // members
    base = half_start(lax.axis_index("tm"), own_rows)
    copies = []
    for k, s in enumerate(group):
        offset = half_start(lax.axis_index("chan") ^ s, block)
        rows = pl.ds(offset, block)
        inverse = inverse_ref[pl.ds(pl.multiple_of(base + offset, block), block), :]
        jones = q_ref[rows, :] + rates * inverse * received[k][0:block].astype(F32)
        jones_ref[k] = jones
        duals_ref[k] = u_ref[rows, :] + jones - received[k][block : 2 * block].astype(F32)
        for i, (src, dst) in enumerate(((jones_ref, jones_hbm), (duals_ref, duals_hbm))):
            copies.append(pltpu.make_async_copy(src.at[k], dst.at[rows, :], sems.at[i, k]))
            copies[-1].start()
    for copy in copies:
        copy.wait()


def shape_of(shape, dtype=F32):
    return jax.ShapeDtypeStruct(shape, dtype)


def in_vmem(shape, dtype=F32):
    return pltpu.VMEM(shape, dtype)


def call(kernel, outs, ins, limit, scratch=(), aliases={}, out_space=pltpu.VMEM):
    return pl.pallas_call(
        kernel, out_shape=tuple(outs), in_specs=[pl.BlockSpec(memory_space=space) for space in ins],
        out_specs=tuple(pl.BlockSpec(memory_space=out_space) for _ in outs), scratch_shapes=scratch,
        input_output_aliases=aliases,
        compiler_params=pltpu.CompilerParams(vmem_limit_bytes=limit * MIB),
    )


PIECES = 8
PARTS = (2, 2, 2, 1, 1)
CHUNKS = 2
EARLY = 3


def partner_order(members):
    return list(range(members - 1, 0, -1))


def on_device(residuals, flag_masks, cluster, penalty, jones_init, duals_init):
    members, halves = lax.axis_size("chan"), lax.axis_size("tm")
    share, rows = residuals.shape[1], residuals.shape[3]
    slots, cols = flag_masks.shape[1], jones_init.shape[2]
    own_rows = rows // halves
    block = own_rows // members
    vmem, hbm = pltpu.VMEM, pltpu.HBM
    bf16 = jnp.bfloat16

    resid, grad, sent, masks, counts, inverse, rates, duals0 = call(
        first_kernel,
        [
            in_vmem(residuals.shape[1:], bf16), in_vmem((rows, cols)), in_vmem((rows, cols), WIRE), in_vmem((share, rows, LANES)),
            in_vmem((rows, LANES)), in_vmem((rows, cols)), in_vmem((8, cols)), in_vmem((own_rows, cols)),
        ],
        [hbm] * 6, 40,
        [
            vmem((slots, rows // 2), jnp.int32), vmem((1, cluster.shape[0]), jnp.int32),
            vmem((1, penalty.shape[0]), F32), vmem((rows, cols), F32), vmem((2 * share, rows, cols), bf16),
            pltpu.SemaphoreType.DMA((5 + len(PARTS),)),
        ],
    )(*(
        pltpu.with_memory_space_constraint(x, hbm)
        for x in (residuals[0], flag_masks[0], cluster[None, :], penalty[None, :], jones_init[0], duals_init[0])
    ))

    swap = [(0, 1), (1, 0)]
    grad_other = lax.ppermute(sent, "tm", swap)
    u, other, xs = call(
        functools.partial(other_kernel, CHUNKS),
        [in_vmem((own_rows, cols)), in_vmem((own_rows, cols)), in_vmem((2 * share, rows, cols), bf16)],
        [vmem] * 6, 24,
    )(resid, grad, grad_other, masks, inverse, duals0)
    theirs = lax.ppermute(other, "tm", swap)
    message = in_vmem((2 * block + TILE, cols), WIRE)
    own, *messages = call(
        functools.partial(own_kernel, CHUNKS, members),
        [in_vmem((own_rows, cols))] + [message] * members, [vmem] * 5, 24,
    )(resid, xs, masks, u, counts)
    q, *messages = call(
        functools.partial(pack_kernel, members), [in_vmem((own_rows, cols))] + [message] * members,
        [vmem] * (5 + members), 16, aliases={5 + s: 1 + s for s in range(members)},
    )(own, theirs, u, inverse, rates, *messages)

    def exchange(parts):
        got = [None] * members
        got[0] = parts[0]
        for s in partner_order(members):
            got[s] = lax.ppermute(parts[s], "chan", [(f, f ^ s) for f in range(members)])
        return got

    messages = exchange(messages)
    returned = call(
        functools.partial(owner_kernel, members, block, slots),
        [shape_of((2 * block, cols), WIRE)] * members, [vmem] * (1 + members), 16,
    )(rates, *messages)
    returned = exchange(returned)
    order = [0] + partner_order(members)
    early = len(order) * EARLY // 8
    outputs = []
    for group in (order[:early], order[early:]):
        spaces = [vmem] * (4 + len(group)) + [hbm] * len(outputs)
        outputs = call(
            functools.partial(finish_kernel, members, group),
            [shape_of((own_rows, cols))] * 2, spaces, 16,
            [
                vmem((len(group), block, cols), F32), vmem((len(group), block, cols), F32),
                pltpu.SemaphoreType.DMA((2, len(group))),
            ],
            {4 + len(group) + i: i for i in range(len(outputs))}, hbm,
        )(q, u, inverse, rates, *(returned[s] for s in group), *outputs)
    return outputs[0][None], outputs[1][None]


def solution(mesh):
    in_specs = (
        P(("obs", "chan"), "tm", None, None, None),
        P(("obs", "chan"), None, None),
        P("obs"),
        P("obs"),
        P(("obs", "chan"), None, None),
        P(("obs", "chan"), None, None),
    )
    out_specs = (P(("obs", "chan"), "tm", None), P(("obs", "chan"), "tm", None))
    return jax.shard_map(
        on_device, mesh=mesh, in_specs=in_specs, out_specs=out_specs, check_vma=False
    )
```

profile of v0, /device:TPU:0, one launch (start us, length us, event | category | flops | bytes accessed | tf_op | source)
XLA Modules:
  0.0 50.4 jit_solution(16271499919890007515)
XLA Ops:
  0.6 5.7 %shard_map.77 = (bf16[2,2,1024,1024]{3,2,1,0:T(8,128)(2,1)S(1)}, f32[1024,256]{1,0:T(8,128)S(1)}, bf16[1024,256]{1,0:T(8,128)(2,1)S(1)}, f32[2,1024,128]{2,1,0:T...) custom-call(bf16[2,2,1024,1024]{3,2,1,0:T(8,128)(2,1)} %bitcast.8, ...), custom_call_target="tpu_custom_call" | custom-call | tf_op jit(solution)/shard_map/pallas_call | solution.py:288
  6.3 0.5 %collective-permute-start = (bf16[1024,256]{1,0:T(8,128)(2,1)S(1)}, bf16[1024,256]{1,0:T(8,128)(2,1)S(1)}, u32[]{:S(2)}, u32[]{:S(2)}) collective-permute-start(bf16[1024,256]{1,0:T(8,128)(2,1)S(1)} %get-tuple-element.45), channel_id=1, source_target_pairs={{0,1},{1,0},{2,3},{3,2},{4,5},{5,4},{6,7},{7,6},{8,9},{9,8},{10,11... | collective-permute-start | bytes 1572872 | tf_op jit(solution)/shard_map/ppermute | solution.py:306
  6.9 1.5 %collective-permute-done.theirs_ref = bf16[1024,256]{1,0:T(8,128)(2,1)S(1)} collective-permute-done((bf16[1024,256]{1,0:T(8,128)(2,1)S(1)}, bf16[1024,256]{1,0:T(8,128)(2,1)S(1)}, u32[]{:S(2)}, u32[]{:S(2)}) %collective-permute-start) | collective-permute-done | bytes 524320 | tf_op jit(solution)/shard_map/ppermute | solution.py:306
  8.4 1.4 %shard_map.78 = (f32[512,256]{1,0:T(8,128)S(1)}, f32[512,256]{1,0:T(8,128)S(1)}, bf16[4,1024,256]{2,1,0:T(8,128)(2,1)S(1)}) custom-call(bf16[2,2,1024,1024]{3,2,1,0:T(8,128)(2,1)S(1)} %get-tuple-element.43.resid_ref, f32[1024,256]{1,0:T(8,128)S(1)} %get-tuple-element.44.mine_ref, bf16[1024,256]{1,0:T(8,128)(2,1)S(1)} %collective-permute-done.theirs_ref, ...), custom_call_target="tpu_custom_call" | custom-call | tf_op jit(solution)/shard_map/pallas_call | solution.py:307
  9.8 0.4 collective-permute-start.1
  10.3 1.3 %shard_map.79 = (f32[512,256]{1,0:T(8,128)S(1)}, bf16[136,256]{1,0:T(8,128)(2,1)S(1)}, bf16[136,256]{1,0:T(8,128)(2,1)S(1)}, bf16[136,256]{1,0:T(8,128)(2,1)S(1)...) custom-call(bf16[2,2,1024,1024]{3,2,1,0:T(8,128)(2,1)S(1)} %get-tupl, ...), custom_call_target="tpu_custom_call" | custom-call | tf_op jit(solution)/shard_map/pallas_call | solution.py:314
  11.6 0.3 collective-permute-done.1.theirs_ref
  11.8 0.2 shard_map.80
  12.0 2.9 %collective-permute-start.2 = (bf16[136,256]{1,0:T(8,128)(2,1)S(1)}, bf16[136,256]{1,0:T(8,128)(2,1)S(1)}, u32[]{:S(2)}, u32[]{:S(2)}) collective-permute-start(bf16[136,256]{1,0:T(8,128)(2,1)S(1)} %get-tuple-element.65), channel_id=1, source_target_pairs={{0,2},{2,0},{4,6},{6,4},{8,10},{10,8},{12,14},{14,12},{1,3},{3,1},... | collective-permute-start | bytes 208904 | tf_op jit(solution)/shard_map/ppermute | solution.py:327
  14.9 1.6 %collective-permute-start.3 = (bf16[136,256]{1,0:T(8,128)(2,1)S(1)}, bf16[136,256]{1,0:T(8,128)(2,1)S(1)}, u32[]{:S(2)}, u32[]{:S(2)}) collective-permute-start(bf16[136,256]{1,0:T(8,128)(2,1)S(1)} %get-tuple-element.66), channel_id=1, source_target_pairs={{0,4},{2,6},{4,0},{6,2},{8,12},{10,14},{12,8},{14,10},{1,5},{3,7},... | collective-permute-start | bytes 208904 | tf_op jit(solution)/shard_map/ppermute | solution.py:327
  16.5 0.0 collective-permute-start.4
  16.5 3.0 %collective-permute-start.5 = (bf16[136,256]{1,0:T(8,128)(2,1)S(1)}, bf16[136,256]{1,0:T(8,128)(2,1)S(1)}, u32[]{:S(2)}, u32[]{:S(2)}) collective-permute-start(bf16[136,256]{1,0:T(8,128)(2,1)S(1)} %get-tuple-element.68), channel_id=1, source_target_pairs={{0,8},{2,10},{4,12},{6,14},{8,0},{10,2},{12,4},{14,6},{1,9},{3,11}... | collective-permute-start | bytes 208904 | tf_op jit(solution)/shard_map/ppermute | solution.py:327
  19.5 1.3 %collective-permute-start.6 = (bf16[136,256]{1,0:T(8,128)(2,1)S(1)}, bf16[136,256]{1,0:T(8,128)(2,1)S(1)}, u32[]{:S(2)}, u32[]{:S(2)}) collective-permute-start(bf16[136,256]{1,0:T(8,128)(2,1)S(1)} %get-tuple-element.69), channel_id=1, source_target_pairs={{0,10},{2,8},{4,14},{6,12},{8,2},{10,0},{12,6},{14,4},{1,11},{3,9}... | collective-permute-start | bytes 208904 | tf_op jit(solution)/shard_map/ppermute | solution.py:327
  20.8 3.6 %collective-permute-start.7 = (bf16[136,256]{1,0:T(8,128)(2,1)S(1)}, bf16[136,256]{1,0:T(8,128)(2,1)S(1)}, u32[]{:S(2)}, u32[]{:S(2)}) collective-permute-start(bf16[136,256]{1,0:T(8,128)(2,1)S(1)} %get-tuple-element.70), channel_id=1, source_target_pairs={{0,12},{2,14},{4,8},{6,10},{8,4},{10,6},{12,0},{14,2},{1,13},{3,15... | collective-permute-start | bytes 208904 | tf_op jit(solution)/shard_map/ppermute | solution.py:327
  24.4 0.0 collective-permute-done.5.refs_4_
  24.4 5.9 %collective-permute-done.6.refs_5_ = bf16[136,256]{1,0:T(8,128)(2,1)S(1)} collective-permute-done((bf16[136,256]{1,0:T(8,128)(2,1)S(1)}, bf16[136,256]{1,0:T(8,128)(2,1)S(1)}, u32[]{:S(2)}, u32[]{:S(2)}) %collective-permute-start.6) | collective-permute-done | bytes 69664 | tf_op jit(solution)/shard_map/ppermute | solution.py:327
  30.4 1.2 %collective-permute-done.8.refs_7_ = bf16[136,256]{1,0:T(8,128)(2,1)S(1)} collective-permute-done((bf16[136,256]{1,0:T(8,128)(2,1)S(1)}, bf16[136,256]{1,0:T(8,128)(2,1)S(1)}, u32[]{:S(2)}, u32[]{:S(2)}) %collective-permute-start.8) | collective-permute-done | bytes 69664 | tf_op jit(solution)/shard_map/ppermute | solution.py:327
  31.5 0.7 %shard_map.81 = (bf16[128,256]{1,0:T(8,128)(2,1)S(1)}, bf16[128,256]{1,0:T(8,128)(2,1)S(1)}, bf16[128,256]{1,0:T(8,128)(2,1)S(1)}, bf16[128,256]{1,0:T(8,128)(2,...) custom-call(f32[8,256]{1,0:T(8,128)S(1)} %get-tuple-element.54.rates, ...), custom_call_target="tpu_custom_call" | custom-call | tf_op jit(solution)/shard_map/pallas_call | solution.py:331
  32.2 2.3 %collective-permute-start.14 = (bf16[128,256]{1,0:T(8,128)(2,1)S(1)}, bf16[128,256]{1,0:T(8,128)(2,1)S(1)}, u32[]{:S(2)}, u32[]{:S(2)}) collective-permute-start(bf16[128,256]{1,0:T(8,128)(2,1)S(1)} %get-tuple-element.78), channel_id=1, source_target_pairs={{0,14},{2,12},{4,10},{6,8},{8,6},{10,4},{12,2},{14,0},{1,15},{3,13... | collective-permute-start | bytes 196616 | tf_op jit(solution)/shard_map/ppermute | solution.py:327
  34.5 1.6 %collective-permute-start.15 = (bf16[128,256]{1,0:T(8,128)(2,1)S(1)}, bf16[128,256]{1,0:T(8,128)(2,1)S(1)}, u32[]{:S(2)}, u32[]{:S(2)}) collective-permute-start(bf16[128,256]{1,0:T(8,128)(2,1)S(1)} %get-tuple-element.79), channel_id=1, source_target_pairs={{0,12},{2,14},{4,8},{6,10},{8,4},{10,6},{12,0},{14,2},{1,13},{3,15... | collective-permute-start | bytes 196616 | tf_op jit(solution)/shard_map/ppermute | solution.py:327
  36.0 2.9 %collective-permute-start.9 = (bf16[128,256]{1,0:T(8,128)(2,1)S(1)}, bf16[128,256]{1,0:T(8,128)(2,1)S(1)}, u32[]{:S(2)}, u32[]{:S(2)}) collective-permute-start(bf16[128,256]{1,0:T(8,128)(2,1)S(1)} %get-tuple-element.72), channel_id=1, source_target_pairs={{0,10},{2,8},{4,14},{6,12},{8,2},{10,0},{12,6},{14,4},{1,11},{3,9}... | collective-permute-start | bytes 196616 | tf_op jit(solution)/shard_map/ppermute | solution.py:327
  38.9 1.1 %collective-permute-start.10 = (bf16[128,256]{1,0:T(8,128)(2,1)S(1)}, bf16[128,256]{1,0:T(8,128)(2,1)S(1)}, u32[]{:S(2)}, u32[]{:S(2)}) collective-permute-start(bf16[128,256]{1,0:T(8,128)(2,1)S(1)} %get-tuple-element.73), channel_id=1, source_target_pairs={{0,8},{2,10},{4,12},{6,14},{8,0},{10,2},{12,4},{14,6},{1,9},{3,11}... | collective-permute-start | bytes 196616 | tf_op jit(solution)/shard_map/ppermute | solution.py:327
  39.9 1.1 %collective-permute-start.11 = (bf16[128,256]{1,0:T(8,128)(2,1)S(1)}, bf16[128,256]{1,0:T(8,128)(2,1)S(1)}, u32[]{:S(2)}, u32[]{:S(2)}) collective-permute-start(bf16[128,256]{1,0:T(8,128)(2,1)S(1)} %get-tuple-element.74), channel_id=1, source_target_pairs={{0,6},{2,4},{4,2},{6,0},{8,14},{10,12},{12,10},{14,8},{1,7},{3,5},... | collective-permute-start | bytes 196616 | tf_op jit(solution)/shard_map/ppermute | solution.py:327
  41.0 0.0 collective-permute-done.14.refs_1_
  41.0 4.1 %collective-permute-start.12 = (bf16[128,256]{1,0:T(8,128)(2,1)S(1)}, bf16[128,256]{1,0:T(8,128)(2,1)S(1)}, u32[]{:S(2)}, u32[]{:S(2)}) collective-permute-start(bf16[128,256]{1,0:T(8,128)(2,1)S(1)} %get-tuple-element.75), channel_id=1, source_target_pairs={{0,4},{2,6},{4,0},{6,2},{8,12},{10,14},{12,8},{14,10},{1,5},{3,7},... | collective-permute-start | bytes 196616 | tf_op jit(solution)/shard_map/ppermute | solution.py:327
  45.2 0.0 collective-permute-done.15.refs_2_
  45.2 0.2 collective-permute-start.13
  45.4 0.8 %shard_map.82 = (f32[512,256]{1,0:T(8,128)}, f32[512,256]{1,0:T(8,128)}) custom-call(f32[512,256]{1,0:T(8,128)S(1)} %get-tuple-element.63.q_ref, f32[512,256]{1,0:T(8,128)S(1)} %get-tuple-element.50.u_ref, f32[1024,256]{1,0:T(8,128)S(1)} %get-tuple-element.47.inverse_ref, f32[8,256]{1,0:T(8,128)S(1)} %get-tuple-element.54.rates_ref, ...), custom_call_target="tpu_custom_call" | custom-call | tf_op jit(solution)/shard_map/pallas_call | solution.py:341
  46.2 1.5 %collective-permute-done.9.refs_0_ = bf16[128,256]{1,0:T(8,128)(2,1)S(1)} collective-permute-done((bf16[128,256]{1,0:T(8,128)(2,1)S(1)}, bf16[128,256]{1,0:T(8,128)(2,1)S(1)}, u32[]{:S(2)}, u32[]{:S(2)}) %collective-permute-start.9) | collective-permute-done | bytes 65568 | tf_op jit(solution)/shard_map/ppermute | solution.py:327
  47.7 0.4 collective-permute-done.12.refs_3_
  48.2 1.3 %collective-permute-done.13.refs_4_ = bf16[128,256]{1,0:T(8,128)(2,1)S(1)} collective-permute-done((bf16[128,256]{1,0:T(8,128)(2,1)S(1)}, bf16[128,256]{1,0:T(8,128)(2,1)S(1)}, u32[]{:S(2)}, u32[]{:S(2)}) %collective-permute-start.13) | collective-permute-done | bytes 65568 | tf_op jit(solution)/shard_map/ppermute | solution.py:327
  49.4 0.9 %shard_map.83 = (f32[512,256]{1,0:T(8,128)}, f32[512,256]{1,0:T(8,128)}) custom-call(f32[512,256]{1,0:T(8,128)S(1)} %get-tuple-element.63.q_ref, f32[512,256]{1,0:T(8,128)S(1)} %get-tuple-element.50.u_ref, f32[1024,256]{1,0:T(8,128)S(1)} %get-tuple-element.47.inverse_ref, ...), custom_call_target="tpu_custom_call", output_to_operand_aliasing={{0}: (9, {}), {1}: (10, {})} | custom-call | tf_op jit(solution)/shard_map/pallas_call | solution.py:341
  (7 shorter events, 0.0 us)
Async XLA Ops:
  6.3 2.1 %collective-permute-start = (bf16[1024,256]{1,0:T(8,128)(2,1)S(1)}, bf16[1024,256]{1,0:T(8,128)(2,1)S(1)}, u32[]{:S(2)}, u32[]{:S(2)}) collective-permute-start(bf16[1024,256]{1,0:T(8,128)(2,1)S(1)} %get-tuple-element.45), channel_id=1, source_target_pairs={{0,1},{1,0},{2,3},{3,2},{4,5},{5,4},{6,7},{7,6},{8,9},{9,8},{10,11... | collective-permute-start | bytes 1572872 | tf_op jit(solution)/shard_map/ppermute | solution.py:306
  9.8 2.0 %collective-permute-start.1 = (f32[512,256]{1,0:T(8,128)S(1)}, f32[512,256]{1,0:T(8,128)S(1)}, u32[]{:S(2)}, u32[]{:S(2)}) collective-permute-start(f32[512,256]{1,0:T(8,128)S(1)} %get-tuple-element.53), channel_id=1, source_target_pairs={{0,1},{1,0},{2,3},{3,2},{4,5},{5,4},{6,7},{7,6},{8,9},{9,8},{10,11... | collective-permute-start | bytes 1572872 | tf_op jit(solution)/shard_map/ppermute | solution.py:312
  12.0 8.8 %collective-permute-start.2 = (bf16[136,256]{1,0:T(8,128)(2,1)S(1)}, bf16[136,256]{1,0:T(8,128)(2,1)S(1)}, u32[]{:S(2)}, u32[]{:S(2)}) collective-permute-start(bf16[136,256]{1,0:T(8,128)(2,1)S(1)} %get-tuple-element.65), channel_id=1, source_target_pairs={{0,2},{2,0},{4,6},{6,4},{8,10},{10,8},{12,14},{14,12},{1,3},{3,1},... | collective-permute-start | bytes 208904 | tf_op jit(solution)/shard_map/ppermute | solution.py:327
  14.9 9.5 %collective-permute-start.3 = (bf16[136,256]{1,0:T(8,128)(2,1)S(1)}, bf16[136,256]{1,0:T(8,128)(2,1)S(1)}, u32[]{:S(2)}, u32[]{:S(2)}) collective-permute-start(bf16[136,256]{1,0:T(8,128)(2,1)S(1)} %get-tuple-element.66), channel_id=1, source_target_pairs={{0,4},{2,6},{4,0},{6,2},{8,12},{10,14},{12,8},{14,10},{1,5},{3,7},... | collective-permute-start | bytes 208904 | tf_op jit(solution)/shard_map/ppermute | solution.py:327
  16.5 7.9 %collective-permute-start.4 = (bf16[136,256]{1,0:T(8,128)(2,1)S(1)}, bf16[136,256]{1,0:T(8,128)(2,1)S(1)}, u32[]{:S(2)}, u32[]{:S(2)}) collective-permute-start(bf16[136,256]{1,0:T(8,128)(2,1)S(1)} %get-tuple-element.67), channel_id=1, source_target_pairs={{0,6},{2,4},{4,2},{6,0},{8,14},{10,12},{12,10},{14,8},{1,7},{3,5},... | collective-permute-start | bytes 208904 | tf_op jit(solution)/shard_map/ppermute | solution.py:327
  16.5 7.9 %collective-permute-start.5 = (bf16[136,256]{1,0:T(8,128)(2,1)S(1)}, bf16[136,256]{1,0:T(8,128)(2,1)S(1)}, u32[]{:S(2)}, u32[]{:S(2)}) collective-permute-start(bf16[136,256]{1,0:T(8,128)(2,1)S(1)} %get-tuple-element.68), channel_id=1, source_target_pairs={{0,8},{2,10},{4,12},{6,14},{8,0},{10,2},{12,4},{14,6},{1,9},{3,11}... | collective-permute-start | bytes 208904 | tf_op jit(solution)/shard_map/ppermute | solution.py:327
  19.5 10.8 %collective-permute-start.6 = (bf16[136,256]{1,0:T(8,128)(2,1)S(1)}, bf16[136,256]{1,0:T(8,128)(2,1)S(1)}, u32[]{:S(2)}, u32[]{:S(2)}) collective-permute-start(bf16[136,256]{1,0:T(8,128)(2,1)S(1)} %get-tuple-element.69), channel_id=1, source_target_pairs={{0,10},{2,8},{4,14},{6,12},{8,2},{10,0},{12,6},{14,4},{1,11},{3,9}... | collective-permute-start | bytes 208904 | tf_op jit(solution)/shard_map/ppermute | solution.py:327
  20.8 9.6 %collective-permute-start.7 = (bf16[136,256]{1,0:T(8,128)(2,1)S(1)}, bf16[136,256]{1,0:T(8,128)(2,1)S(1)}, u32[]{:S(2)}, u32[]{:S(2)}) collective-permute-start(bf16[136,256]{1,0:T(8,128)(2,1)S(1)} %get-tuple-element.70), channel_id=1, source_target_pairs={{0,12},{2,14},{4,8},{6,10},{8,4},{10,6},{12,0},{14,2},{1,13},{3,15... | collective-permute-start | bytes 208904 | tf_op jit(solution)/shard_map/ppermute | solution.py:327
  24.4 7.1 %collective-permute-start.8 = (bf16[136,256]{1,0:T(8,128)(2,1)S(1)}, bf16[136,256]{1,0:T(8,128)(2,1)S(1)}, u32[]{:S(2)}, u32[]{:S(2)}) collective-permute-start(bf16[136,256]{1,0:T(8,128)(2,1)S(1)} %get-tuple-element.71), channel_id=1, source_target_pairs={{0,14},{2,12},{4,10},{6,8},{8,6},{10,4},{12,2},{14,0},{1,15},{3,13... | collective-permute-start | bytes 208904 | tf_op jit(solution)/shard_map/ppermute | solution.py:327
  32.2 8.8 %collective-permute-start.14 = (bf16[128,256]{1,0:T(8,128)(2,1)S(1)}, bf16[128,256]{1,0:T(8,128)(2,1)S(1)}, u32[]{:S(2)}, u32[]{:S(2)}) collective-permute-start(bf16[128,256]{1,0:T(8,128)(2,1)S(1)} %get-tuple-element.78), channel_id=1, source_target_pairs={{0,14},{2,12},{4,10},{6,8},{8,6},{10,4},{12,2},{14,0},{1,15},{3,13... | collective-permute-start | bytes 196616 | tf_op jit(solution)/shard_map/ppermute | solution.py:327
  34.5 10.7 %collective-permute-start.15 = (bf16[128,256]{1,0:T(8,128)(2,1)S(1)}, bf16[128,256]{1,0:T(8,128)(2,1)S(1)}, u32[]{:S(2)}, u32[]{:S(2)}) collective-permute-start(bf16[128,256]{1,0:T(8,128)(2,1)S(1)} %get-tuple-element.79), channel_id=1, source_target_pairs={{0,12},{2,14},{4,8},{6,10},{8,4},{10,6},{12,0},{14,2},{1,13},{3,15... | collective-permute-start | bytes 196616 | tf_op jit(solution)/shard_map/ppermute | solution.py:327
  36.0 11.7 %collective-permute-start.9 = (bf16[128,256]{1,0:T(8,128)(2,1)S(1)}, bf16[128,256]{1,0:T(8,128)(2,1)S(1)}, u32[]{:S(2)}, u32[]{:S(2)}) collective-permute-start(bf16[128,256]{1,0:T(8,128)(2,1)S(1)} %get-tuple-element.72), channel_id=1, source_target_pairs={{0,10},{2,8},{4,14},{6,12},{8,2},{10,0},{12,6},{14,4},{1,11},{3,9}... | collective-permute-start | bytes 196616 | tf_op jit(solution)/shard_map/ppermute | solution.py:327
  38.9 8.9 %collective-permute-start.10 = (bf16[128,256]{1,0:T(8,128)(2,1)S(1)}, bf16[128,256]{1,0:T(8,128)(2,1)S(1)}, u32[]{:S(2)}, u32[]{:S(2)}) collective-permute-start(bf16[128,256]{1,0:T(8,128)(2,1)S(1)} %get-tuple-element.73), channel_id=1, source_target_pairs={{0,8},{2,10},{4,12},{6,14},{8,0},{10,2},{12,4},{14,6},{1,9},{3,11}... | collective-permute-start | bytes 196616 | tf_op jit(solution)/shard_map/ppermute | solution.py:327
  39.9 7.8 %collective-permute-start.11 = (bf16[128,256]{1,0:T(8,128)(2,1)S(1)}, bf16[128,256]{1,0:T(8,128)(2,1)S(1)}, u32[]{:S(2)}, u32[]{:S(2)}) collective-permute-start(bf16[128,256]{1,0:T(8,128)(2,1)S(1)} %get-tuple-element.74), channel_id=1, source_target_pairs={{0,6},{2,4},{4,2},{6,0},{8,14},{10,12},{12,10},{14,8},{1,7},{3,5},... | collective-permute-start | bytes 196616 | tf_op jit(solution)/shard_map/ppermute | solution.py:327
  41.0 7.1 %collective-permute-start.12 = (bf16[128,256]{1,0:T(8,128)(2,1)S(1)}, bf16[128,256]{1,0:T(8,128)(2,1)S(1)}, u32[]{:S(2)}, u32[]{:S(2)}) collective-permute-start(bf16[128,256]{1,0:T(8,128)(2,1)S(1)} %get-tuple-element.75), channel_id=1, source_target_pairs={{0,4},{2,6},{4,0},{6,2},{8,12},{10,14},{12,8},{14,10},{1,5},{3,7},... | collective-permute-start | bytes 196616 | tf_op jit(solution)/shard_map/ppermute | solution.py:327
  45.2 4.3 %collective-permute-start.13 = (bf16[128,256]{1,0:T(8,128)(2,1)S(1)}, bf16[128,256]{1,0:T(8,128)(2,1)S(1)}, u32[]{:S(2)}, u32[]{:S(2)}) collective-permute-start(bf16[128,256]{1,0:T(8,128)(2,1)S(1)} %get-tuple-element.76), channel_id=1, source_target_pairs={{0,2},{2,0},{4,6},{6,4},{8,10},{10,8},{12,14},{14,12},{1,3},{3,1},... | collective-permute-start | bytes 196616 | tf_op jit(solution)/shard_map/ppermute | solution.py:327
where the time goes:
time: 50.6 us; the launch traced here: 50.4 us
  starting transfers between devices  26.5 us (52%)
  waiting for transfers between devices  12.1 us (24%)
  Pallas kernels  11 us (22%)
  between operations  0.7 us (1%)
    ppermute x14, starting transfers between devices, exchange(): lax.ppermute(parts[s], 'chan', [(f, f ^ s) for f in range(members)])  25.6 us
    ppermute x14, waiting for transfers between devices, exchange(): lax.ppermute(parts[s], 'chan', [(f, f ^ s) for f in range(members)])  10.3 us
    pallas_call x1, Pallas kernels, on_device(): call(first_kernel, [in_vmem(residuals.shape[1:], bf16), in_vmem((rows, co...  5.66 us
    pallas_call x2, Pallas kernels, on_device(): call(functools.partial(finish_kernel, members, group), [shape_of((own_row...  1.74 us
    ppermute x1, waiting for transfers between devices, on_device(): grad_other = lax.ppermute(sent, 'tm', swap)  1.54 us
    pallas_call x1, Pallas kernels, on_device(): call(functools.partial(other_kernel, CHUNKS), [in_vmem((own_rows, cols)),...  1.44 us
    pallas_call x1, Pallas kernels, on_device(): call(functools.partial(own_kernel, CHUNKS, members), [in_vmem((own_rows,...  1.27 us
  transfers between devices with their start and end apart: 16, of which 7 were waited for; matrix products, arithmetic and copies ran while one was open for 0% of the time, Pallas kernels for 4%

commit v1 on v0

--- a/solution.py
+++ b/solution.py
@@ -64,6 +64,17 @@
         part = twice(mask_ref[t, rows, :]) * product
         total = part if total is None else total + part
     return total
+
+
+def store_wide(message, first, block, value):
+    for k in range(value.shape[1] // LANES):
+        message[first + k * block : first + (k + 1) * block] = value[:, k * LANES : (k + 1) * LANES].astype(WIRE)
+
+
+def load_wide(message, first, block, cols):
+    return jnp.concatenate(
+        [message[first + k * block : first + (k + 1) * block].astype(F32) for k in range(cols // LANES)], axis=1
+    )
 
 
 def half_start(index, rows):
@@ -170,10 +181,11 @@
     eye = eye_mask(block)
     for s, message in enumerate(message_refs):
         offset = half_start(lax.axis_index("chan") ^ s, block)
-        message[0:block] = u_ref[pl.ds(offset, block), :].astype(WIRE)
+        store_wide(message, 0, block, u_ref[pl.ds(offset, block), :])
         counts = counts_ref[pl.ds(pl.multiple_of(base + offset, block), block), :]
         line = jnp.sum(jnp.where(eye, counts, 0.0), axis=0, keepdims=True)
-        message[2 * block : 2 * block + TILE, 0:LANES] = jnp.broadcast_to(line, (TILE, LANES)).astype(WIRE)
+        first = 2 * block * (u_ref.shape[1] // LANES)
+        message[first : first + TILE] = jnp.broadcast_to(line, (TILE, LANES)).astype(WIRE)
 
 
 def pack_kernel(members, own_ref, theirs_ref, u_ref, inverse_ref, rates_ref, *refs):
@@ -189,12 +201,12 @@
         inverse = inverse_ref[pl.ds(pl.multiple_of(base + offset, block), block), :]
         q = (own_ref[rows, :] + theirs_ref[rows, :] - rates * u) * inverse
         q_ref[rows, :] = q
-        message[block : 2 * block] = (u + q).astype(WIRE)
+        store_wide(message, block * (u.shape[1] // LANES), block, u + q)
 
 
 def owner_kernel(members, block, slots, rates_ref, *refs):
     received, returned = refs[:members], refs[members:]
-    rates = rates_ref[0:1]
+    rates, cols = rates_ref[0:1], rates_ref.shape[1]
     eye = eye_mask(block)
     table = [2.0 * rates / (float(count) + rates) for count in range(slots + 1)]
     weights = [basis_at(lax.axis_index("chan") ^ s, members) for s in range(members)]
@@ -202,13 +214,14 @@
     sums = [None] * POLY
     plus = lambda a, b: b if a is None else a + b
     for s in range(members):
-        u = received[s][0:block].astype(F32)
-        w = received[s][block : 2 * block].astype(F32)
+        u = load_wide(received[s], 0, block, cols)
+        w = load_wide(received[s], block * (cols // LANES), block, cols)
         for p in range(POLY):
             coeffs[p] = plus(coeffs[p], weights[s][p] * u)
             sums[p] = plus(sums[p], weights[s][p] * w)
     for s in range(members):
-        line = received[s][2 * block : 2 * block + TILE, 0:LANES].astype(F32)[0:1]
+        first = 2 * block * (cols // LANES)
+        line = received[s][first : first + TILE].astype(F32)[0:1]
         counts = jnp.sum(jnp.where(eye, line, 0.0), axis=1, keepdims=True)
         first = weights[s][0] * coeffs[0]
         for p in range(1, POLY):
@@ -267,13 +280,15 @@
 
 
 PIECES = 8
-PARTS = (2, 2, 2, 1, 1)
-CHUNKS = 2
+PARTS = (2, 2, 2, 2)
+CHUNKS = 1
 EARLY = 3
 
 
 def partner_order(members):
-    return list(range(members - 1, 0, -1))
+    far = list(range(members - 1, members // 2 - 1, -1))
+    near = list(range(members // 2 - 1, 0, -1))
+    return far[:1] + [partner for pair in zip(far[1:], near) for partner in pair]
 
 
 def on_device(residuals, flag_masks, cluster, penalty, jones_init, duals_init):
@@ -310,7 +325,7 @@
         [vmem] * 6, 24,
     )(resid, grad, grad_other, masks, inverse, duals0)
     theirs = lax.ppermute(other, "tm", swap)
-    message = in_vmem((2 * block + TILE, cols), WIRE)
+    message = in_vmem((2 * block * (cols // LANES) + TILE, LANES), WIRE)
     own, *messages = call(
         functools.partial(own_kernel, CHUNKS, members),
         [in_vmem((own_rows, cols))] + [message] * members, [vmem] * 5, 24,

time: 50.6 us -> 48 us (0.949)
  starting transfers between devices: 26.5 us -> 24.6 us
    ppermute x14, starting transfers between devices: 25.6 us -> 23.6 us  [exchange(): lax.ppermute(parts[s], 'chan', [(f, f ^ s) for f in range(members)])]
    pallas_call x1, Pallas kernels: 5.66 us -> 5.15 us  [on_device(): call(first_kernel, [in_vmem(residuals.shape[1:], bf16), in_vmem((rows, co...]
  transfers between devices with their start and end apart: 16 -> 16, of which waited for: 7 -> 5; matrix products, arithmetic and copies ran while one was open for 0% -> 0% of each run, Pallas kernels for 4% -> 4%
where the time goes in v1:
time: 48 us; the launch traced here: 47.8 us
  starting transfers between devices  24.6 us (51%)
  waiting for transfers between devices  12 us (25%)
  Pallas kernels  10.5 us (22%)
  between operations  0.71 us (1%)
    ppermute x14, starting transfers between devices, exchange(): lax.ppermute(parts[s], 'chan', [(f, f ^ s) for f in range(members)])  23.6 us
    ppermute x14, waiting for transfers between devices, exchange(): lax.ppermute(parts[s], 'chan', [(f, f ^ s) for f in range(members)])  10.2 us
    pallas_call x1, Pallas kernels, on_device(): call(first_kernel, [in_vmem(residuals.shape[1:], bf16), in_vmem((rows, co...  5.15 us
    pallas_call x2, Pallas kernels, on_device(): call(functools.partial(finish_kernel, members, group), [shape_of((own_row...  1.75 us
    ppermute x1, waiting for transfers between devices, on_device(): grad_other = lax.ppermute(sent, 'tm', swap)  1.54 us
    pallas_call x1, Pallas kernels, on_device(): call(functools.partial(other_kernel, CHUNKS), [in_vmem((own_rows, cols)),...  1.44 us
    pallas_call x1, Pallas kernels, on_device(): call(functools.partial(own_kernel, CHUNKS, members), [in_vmem((own_rows,...  1.28 us
  transfers between devices with their start and end apart: 16, of which 5 were waited for; matrix products, arithmetic and copies ran while one was open for 0% of the time, Pallas kernels for 4%

profile of v1, /device:TPU:0, one launch (start us, length us, event | category | flops | bytes accessed | tf_op | source)
XLA Modules:
  0.0 47.8 jit_solution(2479841287573321883)
XLA Ops:
  0.6 5.2 %shard_map.77 = (bf16[2,2,1024,1024]{3,2,1,0:T(8,128)(2,1)S(1)}, f32[1024,256]{1,0:T(8,128)S(1)}, bf16[1024,256]{1,0:T(8,128)(2,1)S(1)}, f32[2,1024,128]{2,1,0:T...) custom-call(bf16[2,2,1024,1024]{3,2,1,0:T(8,128)(2,1)} %bitcast.8, ...), custom_call_target="tpu_custom_call" | custom-call | tf_op jit(solution)/shard_map/pallas_call | solution.py:303
  5.8 0.5 %collective-permute-start = (bf16[1024,256]{1,0:T(8,128)(2,1)S(1)}, bf16[1024,256]{1,0:T(8,128)(2,1)S(1)}, u32[]{:S(2)}, u32[]{:S(2)}) collective-permute-start(bf16[1024,256]{1,0:T(8,128)(2,1)S(1)} %get-tuple-element.45), channel_id=1, source_target_pairs={{0,1},{1,0},{2,3},{3,2},{4,5},{5,4},{6,7},{7,6},{8,9},{9,8},{10,11... | collective-permute-start | bytes 1572872 | tf_op jit(solution)/shard_map/ppermute | solution.py:321
  6.3 1.5 %collective-permute-done.theirs_ref = bf16[1024,256]{1,0:T(8,128)(2,1)S(1)} collective-permute-done((bf16[1024,256]{1,0:T(8,128)(2,1)S(1)}, bf16[1024,256]{1,0:T(8,128)(2,1)S(1)}, u32[]{:S(2)}, u32[]{:S(2)}) %collective-permute-start) | collective-permute-done | bytes 524320 | tf_op jit(solution)/shard_map/ppermute | solution.py:321
  7.9 1.4 %shard_map.78 = (f32[512,256]{1,0:T(8,128)S(1)}, f32[512,256]{1,0:T(8,128)S(1)}, bf16[4,1024,256]{2,1,0:T(8,128)(2,1)S(1)}) custom-call(bf16[2,2,1024,1024]{3,2,1,0:T(8,128)(2,1)S(1)} %get-tuple-element.43.resid_ref, f32[1024,256]{1,0:T(8,128)S(1)} %get-tuple-element.44.mine_ref, bf16[1024,256]{1,0:T(8,128)(2,1)S(1)} %collective-permute-done.theirs_ref, ...), custom_call_target="tpu_custom_call" | custom-call | tf_op jit(solution)/shard_map/pallas_call | solution.py:322
  9.3 0.4 collective-permute-start.1
  9.8 1.3 %shard_map.79 = (f32[512,256]{1,0:T(8,128)S(1)}, bf16[264,128]{1,0:T(8,128)(2,1)S(1)}, bf16[264,128]{1,0:T(8,128)(2,1)S(1)}, bf16[264,128]{1,0:T(8,128)(2,1)S(1)...) custom-call(bf16[2,2,1024,1024]{3,2,1,0:T(8,128)(2,1)S(1)} %get-tupl, ...), custom_call_target="tpu_custom_call" | custom-call | tf_op jit(solution)/shard_map/pallas_call | solution.py:329
  11.0 0.3 collective-permute-done.1.theirs_ref
  11.3 0.2 shard_map.80
  11.5 2.9 %collective-permute-start.2 = (bf16[264,128]{1,0:T(8,128)(2,1)S(1)}, bf16[264,128]{1,0:T(8,128)(2,1)S(1)}, u32[]{:S(2)}, u32[]{:S(2)}) collective-permute-start(bf16[264,128]{1,0:T(8,128)(2,1)S(1)} %get-tuple-element.65), channel_id=1, source_target_pairs={{0,2},{2,0},{4,6},{6,4},{8,10},{10,8},{12,14},{14,12},{1,3},{3,1},... | collective-permute-start | bytes 202760 | tf_op jit(solution)/shard_map/ppermute | solution.py:342
  14.4 1.6 %collective-permute-start.3 = (bf16[264,128]{1,0:T(8,128)(2,1)S(1)}, bf16[264,128]{1,0:T(8,128)(2,1)S(1)}, u32[]{:S(2)}, u32[]{:S(2)}) collective-permute-start(bf16[264,128]{1,0:T(8,128)(2,1)S(1)} %get-tuple-element.66), channel_id=1, source_target_pairs={{0,4},{2,6},{4,0},{6,2},{8,12},{10,14},{12,8},{14,10},{1,5},{3,7},... | collective-permute-start | bytes 202760 | tf_op jit(solution)/shard_map/ppermute | solution.py:342
  16.0 0.0 collective-permute-start.4
  16.0 3.0 %collective-permute-start.5 = (bf16[264,128]{1,0:T(8,128)(2,1)S(1)}, bf16[264,128]{1,0:T(8,128)(2,1)S(1)}, u32[]{:S(2)}, u32[]{:S(2)}) collective-permute-start(bf16[264,128]{1,0:T(8,128)(2,1)S(1)} %get-tuple-element.68), channel_id=1, source_target_pairs={{0,8},{2,10},{4,12},{6,14},{8,0},{10,2},{12,4},{14,6},{1,9},{3,11}... | collective-permute-start | bytes 202760 | tf_op jit(solution)/shard_map/ppermute | solution.py:342
  19.0 1.3 %collective-permute-start.6 = (bf16[264,128]{1,0:T(8,128)(2,1)S(1)}, bf16[264,128]{1,0:T(8,128)(2,1)S(1)}, u32[]{:S(2)}, u32[]{:S(2)}) collective-permute-start(bf16[264,128]{1,0:T(8,128)(2,1)S(1)} %get-tuple-element.69), channel_id=1, source_target_pairs={{0,10},{2,8},{4,14},{6,12},{8,2},{10,0},{12,6},{14,4},{1,11},{3,9}... | collective-permute-start | bytes 202760 | tf_op jit(solution)/shard_map/ppermute | solution.py:342
  20.3 3.6 %collective-permute-start.7 = (bf16[264,128]{1,0:T(8,128)(2,1)S(1)}, bf16[264,128]{1,0:T(8,128)(2,1)S(1)}, u32[]{:S(2)}, u32[]{:S(2)}) collective-permute-start(bf16[264,128]{1,0:T(8,128)(2,1)S(1)} %get-tuple-element.70), channel_id=1, source_target_pairs={{0,12},{2,14},{4,8},{6,10},{8,4},{10,6},{12,0},{14,2},{1,13},{3,15... | collective-permute-start | bytes 202760 | tf_op jit(solution)/shard_map/ppermute | solution.py:342
  23.9 0.0 collective-permute-done.3.refs_2_
  23.9 0.0 collective-permute-done.5.refs_4_
  23.9 5.7 %collective-permute-done.6.refs_5_ = bf16[264,128]{1,0:T(8,128)(2,1)S(1)} collective-permute-done((bf16[264,128]{1,0:T(8,128)(2,1)S(1)}, bf16[264,128]{1,0:T(8,128)(2,1)S(1)}, u32[]{:S(2)}, u32[]{:S(2)}) %collective-permute-start.6) | collective-permute-done | bytes 67616 | tf_op jit(solution)/shard_map/ppermute | solution.py:342
  29.6 1.3 %collective-permute-done.8.refs_7_ = bf16[264,128]{1,0:T(8,128)(2,1)S(1)} collective-permute-done((bf16[264,128]{1,0:T(8,128)(2,1)S(1)}, bf16[264,128]{1,0:T(8,128)(2,1)S(1)}, u32[]{:S(2)}, u32[]{:S(2)}) %collective-permute-start.8) | collective-permute-done | bytes 67616 | tf_op jit(solution)/shard_map/ppermute | solution.py:342
  31.0 0.7 %shard_map.81 = (bf16[128,256]{1,0:T(8,128)(2,1)S(1)}, bf16[128,256]{1,0:T(8,128)(2,1)S(1)}, bf16[128,256]{1,0:T(8,128)(2,1)S(1)}, bf16[128,256]{1,0:T(8,128)(2,...) custom-call(f32[8,256]{1,0:T(8,128)S(1)} %get-tuple-element.54.rates, ...), custom_call_target="tpu_custom_call" | custom-call | tf_op jit(solution)/shard_map/pallas_call | solution.py:346
  31.7 1.9 %collective-permute-start.14 = (bf16[128,256]{1,0:T(8,128)(2,1)S(1)}, bf16[128,256]{1,0:T(8,128)(2,1)S(1)}, u32[]{:S(2)}, u32[]{:S(2)}) collective-permute-start(bf16[128,256]{1,0:T(8,128)(2,1)S(1)} %get-tuple-element.78), channel_id=1, source_target_pairs={{0,14},{2,12},{4,10},{6,8},{8,6},{10,4},{12,2},{14,0},{1,15},{3,13... | collective-permute-start | bytes 196616 | tf_op jit(solution)/shard_map/ppermute | solution.py:342
  33.6 1.9 %collective-permute-start.15 = (bf16[128,256]{1,0:T(8,128)(2,1)S(1)}, bf16[128,256]{1,0:T(8,128)(2,1)S(1)}, u32[]{:S(2)}, u32[]{:S(2)}) collective-permute-start(bf16[128,256]{1,0:T(8,128)(2,1)S(1)} %get-tuple-element.79), channel_id=1, source_target_pairs={{0,12},{2,14},{4,8},{6,10},{8,4},{10,6},{12,0},{14,2},{1,13},{3,15... | collective-permute-start | bytes 196616 | tf_op jit(solution)/shard_map/ppermute | solution.py:342
  35.5 1.4 %collective-permute-start.9 = (bf16[128,256]{1,0:T(8,128)(2,1)S(1)}, bf16[128,256]{1,0:T(8,128)(2,1)S(1)}, u32[]{:S(2)}, u32[]{:S(2)}) collective-permute-start(bf16[128,256]{1,0:T(8,128)(2,1)S(1)} %get-tuple-element.72), channel_id=1, source_target_pairs={{0,6},{2,4},{4,2},{6,0},{8,14},{10,12},{12,10},{14,8},{1,7},{3,5},... | collective-permute-start | bytes 196616 | tf_op jit(solution)/shard_map/ppermute | solution.py:342
  36.9 2.0 %collective-permute-start.10 = (bf16[128,256]{1,0:T(8,128)(2,1)S(1)}, bf16[128,256]{1,0:T(8,128)(2,1)S(1)}, u32[]{:S(2)}, u32[]{:S(2)}) collective-permute-start(bf16[128,256]{1,0:T(8,128)(2,1)S(1)} %get-tuple-element.73), channel_id=1, source_target_pairs={{0,10},{2,8},{4,14},{6,12},{8,2},{10,0},{12,6},{14,4},{1,11},{3,9}... | collective-permute-start | bytes 196616 | tf_op jit(solution)/shard_map/ppermute | solution.py:342
  38.9 1.1 %collective-permute-start.11 = (bf16[128,256]{1,0:T(8,128)(2,1)S(1)}, bf16[128,256]{1,0:T(8,128)(2,1)S(1)}, u32[]{:S(2)}, u32[]{:S(2)}) collective-permute-start(bf16[128,256]{1,0:T(8,128)(2,1)S(1)} %get-tuple-element.74), channel_id=1, source_target_pairs={{0,4},{2,6},{4,0},{6,2},{8,12},{10,14},{12,8},{14,10},{1,5},{3,7},... | collective-permute-start | bytes 196616 | tf_op jit(solution)/shard_map/ppermute | solution.py:342
  40.0 0.0 collective-permute-done.14.refs_1_
  40.0 1.4 %collective-permute-start.12 = (bf16[128,256]{1,0:T(8,128)(2,1)S(1)}, bf16[128,256]{1,0:T(8,128)(2,1)S(1)}, u32[]{:S(2)}, u32[]{:S(2)}) collective-permute-start(bf16[128,256]{1,0:T(8,128)(2,1)S(1)} %get-tuple-element.75), channel_id=1, source_target_pairs={{0,8},{2,10},{4,12},{6,14},{8,0},{10,2},{12,4},{14,6},{1,9},{3,11}... | collective-permute-start | bytes 196616 | tf_op jit(solution)/shard_map/ppermute | solution.py:342
  41.4 0.0 collective-permute-done.15.refs_2_
  41.4 1.5 %collective-permute-start.13 = (bf16[128,256]{1,0:T(8,128)(2,1)S(1)}, bf16[128,256]{1,0:T(8,128)(2,1)S(1)}, u32[]{:S(2)}, u32[]{:S(2)}) collective-permute-start(bf16[128,256]{1,0:T(8,128)(2,1)S(1)} %get-tuple-element.76), channel_id=1, source_target_pairs={{0,2},{2,0},{4,6},{6,4},{8,10},{10,8},{12,14},{14,12},{1,3},{3,1},... | collective-permute-start | bytes 196616 | tf_op jit(solution)/shard_map/ppermute | solution.py:342
  42.9 0.8 %shard_map.82 = (f32[512,256]{1,0:T(8,128)}, f32[512,256]{1,0:T(8,128)}) custom-call(f32[512,256]{1,0:T(8,128)S(1)} %get-tuple-element.63.q_ref, f32[512,256]{1,0:T(8,128)S(1)} %get-tuple-element.50.u_ref, f32[1024,256]{1,0:T(8,128)S(1)} %get-tuple-element.47.inverse_ref, f32[8,256]{1,0:T(8,128)S(1)} %get-tuple-element.54.rates_ref, ...), custom_call_target="tpu_custom_call" | custom-call | tf_op jit(solution)/shard_map/pallas_call | solution.py:356
  43.7 3.1 %collective-permute-done.10.refs_1_ = bf16[128,256]{1,0:T(8,128)(2,1)S(1)} collective-permute-done((bf16[128,256]{1,0:T(8,128)(2,1)S(1)}, bf16[128,256]{1,0:T(8,128)(2,1)S(1)}, u32[]{:S(2)}, u32[]{:S(2)}) %collective-permute-start.10) | collective-permute-done | bytes 65568 | tf_op jit(solution)/shard_map/ppermute | solution.py:342
  46.8 0.0 collective-permute-done.11.refs_2_
  46.9 0.9 %shard_map.83 = (f32[512,256]{1,0:T(8,128)}, f32[512,256]{1,0:T(8,128)}) custom-call(f32[512,256]{1,0:T(8,128)S(1)} %get-tuple-element.63.q_ref, f32[512,256]{1,0:T(8,128)S(1)} %get-tuple-element.50.u_ref, f32[1024,256]{1,0:T(8,128)S(1)} %get-tuple-element.47.inverse_ref, ...), custom_call_target="tpu_custom_call", output_to_operand_aliasing={{0}: (9, {}), {1}: (10, {})} | custom-call | tf_op jit(solution)/shard_map/pallas_call | solution.py:356
  (7 shorter events, 0.0 us)
Async XLA Ops:
  5.8 2.1 %collective-permute-start = (bf16[1024,256]{1,0:T(8,128)(2,1)S(1)}, bf16[1024,256]{1,0:T(8,128)(2,1)S(1)}, u32[]{:S(2)}, u32[]{:S(2)}) collective-permute-start(bf16[1024,256]{1,0:T(8,128)(2,1)S(1)} %get-tuple-element.45), channel_id=1, source_target_pairs={{0,1},{1,0},{2,3},{3,2},{4,5},{5,4},{6,7},{7,6},{8,9},{9,8},{10,11... | collective-permute-start | bytes 1572872 | tf_op jit(solution)/shard_map/ppermute | solution.py:321
  9.3 2.0 %collective-permute-start.1 = (f32[512,256]{1,0:T(8,128)S(1)}, f32[512,256]{1,0:T(8,128)S(1)}, u32[]{:S(2)}, u32[]{:S(2)}) collective-permute-start(f32[512,256]{1,0:T(8,128)S(1)} %get-tuple-element.53), channel_id=1, source_target_pairs={{0,1},{1,0},{2,3},{3,2},{4,5},{5,4},{6,7},{7,6},{8,9},{9,8},{10,11... | collective-permute-start | bytes 1572872 | tf_op jit(solution)/shard_map/ppermute | solution.py:327
  11.5 8.8 %collective-permute-start.2 = (bf16[264,128]{1,0:T(8,128)(2,1)S(1)}, bf16[264,128]{1,0:T(8,128)(2,1)S(1)}, u32[]{:S(2)}, u32[]{:S(2)}) collective-permute-start(bf16[264,128]{1,0:T(8,128)(2,1)S(1)} %get-tuple-element.65), channel_id=1, source_target_pairs={{0,2},{2,0},{4,6},{6,4},{8,10},{10,8},{12,14},{14,12},{1,3},{3,1},... | collective-permute-start | bytes 202760 | tf_op jit(solution)/shard_map/ppermute | solution.py:342
  14.4 9.5 %collective-permute-start.3 = (bf16[264,128]{1,0:T(8,128)(2,1)S(1)}, bf16[264,128]{1,0:T(8,128)(2,1)S(1)}, u32[]{:S(2)}, u32[]{:S(2)}) collective-permute-start(bf16[264,128]{1,0:T(8,128)(2,1)S(1)} %get-tuple-element.66), channel_id=1, source_target_pairs={{0,4},{2,6},{4,0},{6,2},{8,12},{10,14},{12,8},{14,10},{1,5},{3,7},... | collective-permute-start | bytes 202760 | tf_op jit(solution)/shard_map/ppermute | solution.py:342
  16.0 7.9 %collective-permute-start.4 = (bf16[264,128]{1,0:T(8,128)(2,1)S(1)}, bf16[264,128]{1,0:T(8,128)(2,1)S(1)}, u32[]{:S(2)}, u32[]{:S(2)}) collective-permute-start(bf16[264,128]{1,0:T(8,128)(2,1)S(1)} %get-tuple-element.67), channel_id=1, source_target_pairs={{0,6},{2,4},{4,2},{6,0},{8,14},{10,12},{12,10},{14,8},{1,7},{3,5},... | collective-permute-start | bytes 202760 | tf_op jit(solution)/shard_map/ppermute | solution.py:342
  16.0 7.9 %collective-permute-start.5 = (bf16[264,128]{1,0:T(8,128)(2,1)S(1)}, bf16[264,128]{1,0:T(8,128)(2,1)S(1)}, u32[]{:S(2)}, u32[]{:S(2)}) collective-permute-start(bf16[264,128]{1,0:T(8,128)(2,1)S(1)} %get-tuple-element.68), channel_id=1, source_target_pairs={{0,8},{2,10},{4,12},{6,14},{8,0},{10,2},{12,4},{14,6},{1,9},{3,11}... | collective-permute-start | bytes 202760 | tf_op jit(solution)/shard_map/ppermute | solution.py:342
  19.0 10.7 %collective-permute-start.6 = (bf16[264,128]{1,0:T(8,128)(2,1)S(1)}, bf16[264,128]{1,0:T(8,128)(2,1)S(1)}, u32[]{:S(2)}, u32[]{:S(2)}) collective-permute-start(bf16[264,128]{1,0:T(8,128)(2,1)S(1)} %get-tuple-element.69), channel_id=1, source_target_pairs={{0,10},{2,8},{4,14},{6,12},{8,2},{10,0},{12,6},{14,4},{1,11},{3,9}... | collective-permute-start | bytes 202760 | tf_op jit(solution)/shard_map/ppermute | solution.py:342
  20.3 9.4 %collective-permute-start.7 = (bf16[264,128]{1,0:T(8,128)(2,1)S(1)}, bf16[264,128]{1,0:T(8,128)(2,1)S(1)}, u32[]{:S(2)}, u32[]{:S(2)}) collective-permute-start(bf16[264,128]{1,0:T(8,128)(2,1)S(1)} %get-tuple-element.70), channel_id=1, source_target_pairs={{0,12},{2,14},{4,8},{6,10},{8,4},{10,6},{12,0},{14,2},{1,13},{3,15... | collective-permute-start | bytes 202760 | tf_op jit(solution)/shard_map/ppermute | solution.py:342
  23.9 7.1 %collective-permute-start.8 = (bf16[264,128]{1,0:T(8,128)(2,1)S(1)}, bf16[264,128]{1,0:T(8,128)(2,1)S(1)}, u32[]{:S(2)}, u32[]{:S(2)}) collective-permute-start(bf16[264,128]{1,0:T(8,128)(2,1)S(1)} %get-tuple-element.71), channel_id=1, source_target_pairs={{0,14},{2,12},{4,10},{6,8},{8,6},{10,4},{12,2},{14,0},{1,15},{3,13... | collective-permute-start | bytes 202760 | tf_op jit(solution)/shard_map/ppermute | solution.py:342
  31.7 8.4 %collective-permute-start.14 = (bf16[128,256]{1,0:T(8,128)(2,1)S(1)}, bf16[128,256]{1,0:T(8,128)(2,1)S(1)}, u32[]{:S(2)}, u32[]{:S(2)}) collective-permute-start(bf16[128,256]{1,0:T(8,128)(2,1)S(1)} %get-tuple-element.78), channel_id=1, source_target_pairs={{0,14},{2,12},{4,10},{6,8},{8,6},{10,4},{12,2},{14,0},{1,15},{3,13... | collective-permute-start | bytes 196616 | tf_op jit(solution)/shard_map/ppermute | solution.py:342
  33.6 7.8 %collective-permute-start.15 = (bf16[128,256]{1,0:T(8,128)(2,1)S(1)}, bf16[128,256]{1,0:T(8,128)(2,1)S(1)}, u32[]{:S(2)}, u32[]{:S(2)}) collective-permute-start(bf16[128,256]{1,0:T(8,128)(2,1)S(1)} %get-tuple-element.79), channel_id=1, source_target_pairs={{0,12},{2,14},{4,8},{6,10},{8,4},{10,6},{12,0},{14,2},{1,13},{3,15... | collective-permute-start | bytes 196616 | tf_op jit(solution)/shard_map/ppermute | solution.py:342
  35.5 8.2 %collective-permute-start.9 = (bf16[128,256]{1,0:T(8,128)(2,1)S(1)}, bf16[128,256]{1,0:T(8,128)(2,1)S(1)}, u32[]{:S(2)}, u32[]{:S(2)}) collective-permute-start(bf16[128,256]{1,0:T(8,128)(2,1)S(1)} %get-tuple-element.72), channel_id=1, source_target_pairs={{0,6},{2,4},{4,2},{6,0},{8,14},{10,12},{12,10},{14,8},{1,7},{3,5},... | collective-permute-start | bytes 196616 | tf_op jit(solution)/shard_map/ppermute | solution.py:342
  36.9 9.9 %collective-permute-start.10 = (bf16[128,256]{1,0:T(8,128)(2,1)S(1)}, bf16[128,256]{1,0:T(8,128)(2,1)S(1)}, u32[]{:S(2)}, u32[]{:S(2)}) collective-permute-start(bf16[128,256]{1,0:T(8,128)(2,1)S(1)} %get-tuple-element.73), channel_id=1, source_target_pairs={{0,10},{2,8},{4,14},{6,12},{8,2},{10,0},{12,6},{14,4},{1,11},{3,9}... | collective-permute-start | bytes 196616 | tf_op jit(solution)/shard_map/ppermute | solution.py:342
  38.9 8.0 %collective-permute-start.11 = (bf16[128,256]{1,0:T(8,128)(2,1)S(1)}, bf16[128,256]{1,0:T(8,128)(2,1)S(1)}, u32[]{:S(2)}, u32[]{:S(2)}) collective-permute-start(bf16[128,256]{1,0:T(8,128)(2,1)S(1)} %get-tuple-element.74), channel_id=1, source_target_pairs={{0,4},{2,6},{4,0},{6,2},{8,12},{10,14},{12,8},{14,10},{1,5},{3,7},... | collective-permute-start | bytes 196616 | tf_op jit(solution)/shard_map/ppermute | solution.py:342
  40.0 6.8 %collective-permute-start.12 = (bf16[128,256]{1,0:T(8,128)(2,1)S(1)}, bf16[128,256]{1,0:T(8,128)(2,1)S(1)}, u32[]{:S(2)}, u32[]{:S(2)}) collective-permute-start(bf16[128,256]{1,0:T(8,128)(2,1)S(1)} %get-tuple-element.75), channel_id=1, source_target_pairs={{0,8},{2,10},{4,12},{6,14},{8,0},{10,2},{12,4},{14,6},{1,9},{3,11}... | collective-permute-start | bytes 196616 | tf_op jit(solution)/shard_map/ppermute | solution.py:342
  41.4 5.4 %collective-permute-start.13 = (bf16[128,256]{1,0:T(8,128)(2,1)S(1)}, bf16[128,256]{1,0:T(8,128)(2,1)S(1)}, u32[]{:S(2)}, u32[]{:S(2)}) collective-permute-start(bf16[128,256]{1,0:T(8,128)(2,1)S(1)} %get-tuple-element.76), channel_id=1, source_target_pairs={{0,2},{2,0},{4,6},{6,4},{8,10},{10,8},{12,14},{14,12},{1,3},{3,1},... | collective-permute-start | bytes 196616 | tf_op jit(solution)/shard_map/ppermute | solution.py:342

commit v2 on v1

--- a/solution.py
+++ b/solution.py
@@ -69,12 +69,6 @@
 def store_wide(message, first, block, value):
     for k in range(value.shape[1] // LANES):
         message[first + k * block : first + (k + 1) * block] = value[:, k * LANES : (k + 1) * LANES].astype(WIRE)
-
-
-def load_wide(message, first, block, cols):
-    return jnp.concatenate(
-        [message[first + k * block : first + (k + 1) * block].astype(F32) for k in range(cols // LANES)], axis=1
-    )
 
 
 def half_start(index, rows):
@@ -204,46 +198,60 @@
         store_wide(message, block * (u.shape[1] // LANES), block, u + q)
 
 
+def self_share(weights):
+    return sum(weight * weight for weight in weights[1:]) + weights[0] * weights[0]
+
+
 def owner_kernel(members, block, slots, rates_ref, *refs):
     received, returned = refs[:members], refs[members:]
     rates, cols = rates_ref[0:1], rates_ref.shape[1]
     eye = eye_mask(block)
     table = [2.0 * rates / (float(count) + rates) for count in range(slots + 1)]
     weights = [basis_at(lax.axis_index("chan") ^ s, members) for s in range(members)]
-    coeffs = [None] * POLY
-    sums = [None] * POLY
-    plus = lambda a, b: b if a is None else a + b
+    shares = [self_share(weight) for weight in weights]
+    pieces = cols // LANES
+    ends = 2 * block * pieces
+    usable = []
     for s in range(members):
-        u = load_wide(received[s], 0, block, cols)
-        w = load_wide(received[s], block * (cols // LANES), block, cols)
-        for p in range(POLY):
-            coeffs[p] = plus(coeffs[p], weights[s][p] * u)
-            sums[p] = plus(sums[p], weights[s][p] * w)
-    for s in range(members):
-        first = 2 * block * (cols // LANES)
-        line = received[s][first : first + TILE].astype(F32)[0:1]
-        counts = jnp.sum(jnp.where(eye, line, 0.0), axis=1, keepdims=True)
-        first = weights[s][0] * coeffs[0]
-        for p in range(1, POLY):
-            first = first + weights[s][p] * coeffs[p]
-        returned[s][0:block] = first.astype(WIRE)
-        weight = table[0]
-        for count in range(1, slots + 1):
-            weight = jnp.where(counts == count, table[count], weight)
-        step = weight * first
-        for p in range(POLY):
-            sums[p] = sums[p] + weights[s][p] * step
-    for s in range(members):
-        second = weights[s][0] * sums[0]
-        for p in range(1, POLY):
-            second = second + weights[s][p] * sums[p]
-        returned[s][block : 2 * block] = second.astype(WIRE)
+        line = received[s][ends : ends + TILE].astype(F32)[0:1]
+        usable.append(jnp.sum(jnp.where(eye, line, 0.0), axis=1, keepdims=True))
+
+    def combine(terms):
+        total = terms[0]
+        for term in terms[1:]:
+            total = total + term
+        return total
+
+    for row in range(0, block, 2 * TILE):
+        for k in range(pieces):
+            lanes = slice(k * LANES, (k + 1) * LANES)
+            here = slice(k * block + row, k * block + row + 2 * TILE)
+            there = slice((pieces + k) * block + row, (pieces + k) * block + row + 2 * TILE)
+            u = [received[s][here].astype(F32) for s in range(members)]
+            coeffs = [combine([weights[s][p] * u[s] for s in range(members)]) for p in range(POLY)]
+            w = [received[s][there].astype(F32) for s in range(members)]
+            known = []
+            for s in range(members):
+                first = combine([weights[s][p] * coeffs[p] for p in range(POLY)])
+                returned[s][row : row + 2 * TILE, lanes] = (first - shares[s] * u[s]).astype(WIRE)
+                counts = usable[s][row : row + 2 * TILE]
+                weight = table[0][:, lanes]
+                for count in range(1, slots + 1):
+                    weight = jnp.where(counts == count, table[count][:, lanes], weight)
+                step = weight * first
+                known.append(shares[s] * w[s] + step)
+                w[s] = w[s] + step
+            sums = [combine([weights[s][p] * w[s] for s in range(members)]) for p in range(POLY)]
+            for s in range(members):
+                second = combine([weights[s][p] * sums[p] for p in range(POLY)])
+                returned[s][block + row : block + row + 2 * TILE, lanes] = (second - known[s]).astype(WIRE)
 
 
 def finish_kernel(members, group, q_ref, u_ref, inverse_ref, rates_ref, *refs):
     received = refs[: len(group)]
     jones_hbm, duals_hbm, jones_ref, duals_ref, sems = refs[-5:]
     rates = 2.0 * rates_ref[0:1]
+    share = self_share(basis_at(lax.axis_index("chan"), members))
     own_rows = u_ref.shape[0]
     block = own_rows // members
     base = half_start(lax.axis_index("tm"), own_rows)
@@ -252,9 +260,10 @@
         offset = half_start(lax.axis_index("chan") ^ s, block)
         rows = pl.ds(offset, block)
         inverse = inverse_ref[pl.ds(pl.multiple_of(base + offset, block), block), :]
-        jones = q_ref[rows, :] + rates * inverse * received[k][0:block].astype(F32)
-        jones_ref[k] = jones
-        duals_ref[k] = u_ref[rows, :] + jones - received[k][block : 2 * block].astype(F32)
+        u, q = u_ref[rows, :], q_ref[rows, :]
+        first = received[k][0:block].astype(F32) + share * u
+        jones_ref[k] = q + rates * inverse * first
+        duals_ref[k] = (1.0 - share) * (u + q) - received[k][block : 2 * block].astype(F32)
         for i, (src, dst) in enumerate(((jones_ref, jones_hbm), (duals_ref, duals_hbm))):
             copies.append(pltpu.make_async_copy(src.at[k], dst.at[rows, :], sems.at[i, k]))
             copies[-1].start()

time: 48 us -> 48 us (level)
  no operation moved by 1% of the time
where the time goes in v2:
time: 48 us; the launch traced here: 47.8 us
  starting transfers between devices  24.6 us (51%)
  waiting for transfers between devices  12 us (25%)
  Pallas kernels  10.5 us (22%)
  between operations  0.71 us (1%)
    ppermute x14, starting transfers between devices, exchange(): lax.ppermute(parts[s], 'chan', [(f, f ^ s) for f in range(members)])  23.6 us
    ppermute x14, waiting for transfers between devices, exchange(): lax.ppermute(parts[s], 'chan', [(f, f ^ s) for f in range(members)])  10.2 us
    pallas_call x1, Pallas kernels, on_device(): call(first_kernel, [in_vmem(residuals.shape[1:], bf16), in_vmem((rows, co...  5.15 us
    pallas_call x2, Pallas kernels, on_device(): call(functools.partial(finish_kernel, members, group), [shape_of((own_row...  1.78 us
    ppermute x1, waiting for transfers between devices, on_device(): grad_other = lax.ppermute(sent, 'tm', swap)  1.54 us
    pallas_call x1, Pallas kernels, on_device(): call(functools.partial(other_kernel, CHUNKS), [in_vmem((own_rows, cols)),...  1.44 us
    pallas_call x1, Pallas kernels, on_device(): call(functools.partial(own_kernel, CHUNKS, members), [in_vmem((own_rows,...  1.28 us
  transfers between devices with their start and end apart: 16, of which 5 were waited for; matrix products, arithmetic and copies ran while one was open for 0% of the time, Pallas kernels for 4%

profile of v2, /device:TPU:0, one launch (start us, length us, event | category | flops | bytes accessed | tf_op | source)
XLA Modules:
  0.0 47.8 jit_solution(5808959419131118187)
XLA Ops:
  0.6 5.2 %shard_map.77 = (bf16[2,2,1024,1024]{3,2,1,0:T(8,128)(2,1)S(1)}, f32[1024,256]{1,0:T(8,128)S(1)}, bf16[1024,256]{1,0:T(8,128)(2,1)S(1)}, f32[2,1024,128]{2,1,0:T...) custom-call(bf16[2,2,1024,1024]{3,2,1,0:T(8,128)(2,1)} %bitcast.8, ...), custom_call_target="tpu_custom_call" | custom-call | tf_op jit(solution)/shard_map/pallas_call | solution.py:312
  5.8 0.5 %collective-permute-start = (bf16[1024,256]{1,0:T(8,128)(2,1)S(1)}, bf16[1024,256]{1,0:T(8,128)(2,1)S(1)}, u32[]{:S(2)}, u32[]{:S(2)}) collective-permute-start(bf16[1024,256]{1,0:T(8,128)(2,1)S(1)} %get-tuple-element.45), channel_id=1, source_target_pairs={{0,1},{1,0},{2,3},{3,2},{4,5},{5,4},{6,7},{7,6},{8,9},{9,8},{10,11... | collective-permute-start | bytes 1572872 | tf_op jit(solution)/shard_map/ppermute | solution.py:330
  6.3 1.5 %collective-permute-done.theirs_ref = bf16[1024,256]{1,0:T(8,128)(2,1)S(1)} collective-permute-done((bf16[1024,256]{1,0:T(8,128)(2,1)S(1)}, bf16[1024,256]{1,0:T(8,128)(2,1)S(1)}, u32[]{:S(2)}, u32[]{:S(2)}) %collective-permute-start) | collective-permute-done | bytes 524320 | tf_op jit(solution)/shard_map/ppermute | solution.py:330
  7.9 1.4 %shard_map.78 = (f32[512,256]{1,0:T(8,128)S(1)}, f32[512,256]{1,0:T(8,128)S(1)}, bf16[4,1024,256]{2,1,0:T(8,128)(2,1)S(1)}) custom-call(bf16[2,2,1024,1024]{3,2,1,0:T(8,128)(2,1)S(1)} %get-tuple-element.43.resid_ref, f32[1024,256]{1,0:T(8,128)S(1)} %get-tuple-element.44.mine_ref, bf16[1024,256]{1,0:T(8,128)(2,1)S(1)} %collective-permute-done.theirs_ref, ...), custom_call_target="tpu_custom_call" | custom-call | tf_op jit(solution)/shard_map/pallas_call | solution.py:331
  9.3 0.4 collective-permute-start.1
  9.8 1.3 %shard_map.79 = (f32[512,256]{1,0:T(8,128)S(1)}, bf16[264,128]{1,0:T(8,128)(2,1)S(1)}, bf16[264,128]{1,0:T(8,128)(2,1)S(1)}, bf16[264,128]{1,0:T(8,128)(2,1)S(1)...) custom-call(bf16[2,2,1024,1024]{3,2,1,0:T(8,128)(2,1)S(1)} %get-tupl, ...), custom_call_target="tpu_custom_call" | custom-call | tf_op jit(solution)/shard_map/pallas_call | solution.py:338
  11.0 0.3 collective-permute-done.1.theirs_ref
  11.3 0.2 shard_map.80
  11.5 2.9 %collective-permute-start.2 = (bf16[264,128]{1,0:T(8,128)(2,1)S(1)}, bf16[264,128]{1,0:T(8,128)(2,1)S(1)}, u32[]{:S(2)}, u32[]{:S(2)}) collective-permute-start(bf16[264,128]{1,0:T(8,128)(2,1)S(1)} %get-tuple-element.65), channel_id=1, source_target_pairs={{0,2},{2,0},{4,6},{6,4},{8,10},{10,8},{12,14},{14,12},{1,3},{3,1},... | collective-permute-start | bytes 202760 | tf_op jit(solution)/shard_map/ppermute | solution.py:351
  14.4 1.6 %collective-permute-start.3 = (bf16[264,128]{1,0:T(8,128)(2,1)S(1)}, bf16[264,128]{1,0:T(8,128)(2,1)S(1)}, u32[]{:S(2)}, u32[]{:S(2)}) collective-permute-start(bf16[264,128]{1,0:T(8,128)(2,1)S(1)} %get-tuple-element.66), channel_id=1, source_target_pairs={{0,4},{2,6},{4,0},{6,2},{8,12},{10,14},{12,8},{14,10},{1,5},{3,7},... | collective-permute-start | bytes 202760 | tf_op jit(solution)/shard_map/ppermute | solution.py:351
  16.0 0.0 collective-permute-start.4
  16.0 3.0 %collective-permute-start.5 = (bf16[264,128]{1,0:T(8,128)(2,1)S(1)}, bf16[264,128]{1,0:T(8,128)(2,1)S(1)}, u32[]{:S(2)}, u32[]{:S(2)}) collective-permute-start(bf16[264,128]{1,0:T(8,128)(2,1)S(1)} %get-tuple-element.68), channel_id=1, source_target_pairs={{0,8},{2,10},{4,12},{6,14},{8,0},{10,2},{12,4},{14,6},{1,9},{3,11}... | collective-permute-start | bytes 202760 | tf_op jit(solution)/shard_map/ppermute | solution.py:351
  19.0 1.3 %collective-permute-start.6 = (bf16[264,128]{1,0:T(8,128)(2,1)S(1)}, bf16[264,128]{1,0:T(8,128)(2,1)S(1)}, u32[]{:S(2)}, u32[]{:S(2)}) collective-permute-start(bf16[264,128]{1,0:T(8,128)(2,1)S(1)} %get-tuple-element.69), channel_id=1, source_target_pairs={{0,10},{2,8},{4,14},{6,12},{8,2},{10,0},{12,6},{14,4},{1,11},{3,9}... | collective-permute-start | bytes 202760 | tf_op jit(solution)/shard_map/ppermute | solution.py:351
  20.3 3.6 %collective-permute-start.7 = (bf16[264,128]{1,0:T(8,128)(2,1)S(1)}, bf16[264,128]{1,0:T(8,128)(2,1)S(1)}, u32[]{:S(2)}, u32[]{:S(2)}) collective-permute-start(bf16[264,128]{1,0:T(8,128)(2,1)S(1)} %get-tuple-element.70), channel_id=1, source_target_pairs={{0,12},{2,14},{4,8},{6,10},{8,4},{10,6},{12,0},{14,2},{1,13},{3,15... | collective-permute-start | bytes 202760 | tf_op jit(solution)/shard_map/ppermute | solution.py:351
  23.9 0.0 collective-permute-done.3.refs_2_
  23.9 0.0 collective-permute-done.5.refs_4_
  23.9 5.7 %collective-permute-done.6.refs_5_ = bf16[264,128]{1,0:T(8,128)(2,1)S(1)} collective-permute-done((bf16[264,128]{1,0:T(8,128)(2,1)S(1)}, bf16[264,128]{1,0:T(8,128)(2,1)S(1)}, u32[]{:S(2)}, u32[]{:S(2)}) %collective-permute-start.6) | collective-permute-done | bytes 67616 | tf_op jit(solution)/shard_map/ppermute | solution.py:351
  29.6 1.3 %collective-permute-done.8.refs_7_ = bf16[264,128]{1,0:T(8,128)(2,1)S(1)} collective-permute-done((bf16[264,128]{1,0:T(8,128)(2,1)S(1)}, bf16[264,128]{1,0:T(8,128)(2,1)S(1)}, u32[]{:S(2)}, u32[]{:S(2)}) %collective-permute-start.8) | collective-permute-done | bytes 67616 | tf_op jit(solution)/shard_map/ppermute | solution.py:351
  31.0 0.7 %shard_map.81 = (bf16[128,256]{1,0:T(8,128)(2,1)S(1)}, bf16[128,256]{1,0:T(8,128)(2,1)S(1)}, bf16[128,256]{1,0:T(8,128)(2,1)S(1)}, bf16[128,256]{1,0:T(8,128)(2,...) custom-call(f32[8,256]{1,0:T(8,128)S(1)} %get-tuple-element.54.rates, ...), custom_call_target="tpu_custom_call" | custom-call | tf_op jit(solution)/shard_map/pallas_call | solution.py:355
  31.7 1.9 %collective-permute-start.14 = (bf16[128,256]{1,0:T(8,128)(2,1)S(1)}, bf16[128,256]{1,0:T(8,128)(2,1)S(1)}, u32[]{:S(2)}, u32[]{:S(2)}) collective-permute-start(bf16[128,256]{1,0:T(8,128)(2,1)S(1)} %get-tuple-element.78), channel_id=1, source_target_pairs={{0,14},{2,12},{4,10},{6,8},{8,6},{10,4},{12,2},{14,0},{1,15},{3,13... | collective-permute-start | bytes 196616 | tf_op jit(solution)/shard_map/ppermute | solution.py:351
  33.6 1.9 %collective-permute-start.15 = (bf16[128,256]{1,0:T(8,128)(2,1)S(1)}, bf16[128,256]{1,0:T(8,128)(2,1)S(1)}, u32[]{:S(2)}, u32[]{:S(2)}) collective-permute-start(bf16[128,256]{1,0:T(8,128)(2,1)S(1)} %get-tuple-element.79), channel_id=1, source_target_pairs={{0,12},{2,14},{4,8},{6,10},{8,4},{10,6},{12,0},{14,2},{1,13},{3,15... | collective-permute-start | bytes 196616 | tf_op jit(solution)/shard_map/ppermute | solution.py:351
  35.5 1.4 %collective-permute-start.9 = (bf16[128,256]{1,0:T(8,128)(2,1)S(1)}, bf16[128,256]{1,0:T(8,128)(2,1)S(1)}, u32[]{:S(2)}, u32[]{:S(2)}) collective-permute-start(bf16[128,256]{1,0:T(8,128)(2,1)S(1)} %get-tuple-element.72), channel_id=1, source_target_pairs={{0,6},{2,4},{4,2},{6,0},{8,14},{10,12},{12,10},{14,8},{1,7},{3,5},... | collective-permute-start | bytes 196616 | tf_op jit(solution)/shard_map/ppermute | solution.py:351
  36.9 2.0 %collective-permute-start.10 = (bf16[128,256]{1,0:T(8,128)(2,1)S(1)}, bf16[128,256]{1,0:T(8,128)(2,1)S(1)}, u32[]{:S(2)}, u32[]{:S(2)}) collective-permute-start(bf16[128,256]{1,0:T(8,128)(2,1)S(1)} %get-tuple-element.73), channel_id=1, source_target_pairs={{0,10},{2,8},{4,14},{6,12},{8,2},{10,0},{12,6},{14,4},{1,11},{3,9}... | collective-permute-start | bytes 196616 | tf_op jit(solution)/shard_map/ppermute | solution.py:351
  38.9 1.1 %collective-permute-start.11 = (bf16[128,256]{1,0:T(8,128)(2,1)S(1)}, bf16[128,256]{1,0:T(8,128)(2,1)S(1)}, u32[]{:S(2)}, u32[]{:S(2)}) collective-permute-start(bf16[128,256]{1,0:T(8,128)(2,1)S(1)} %get-tuple-element.74), channel_id=1, source_target_pairs={{0,4},{2,6},{4,0},{6,2},{8,12},{10,14},{12,8},{14,10},{1,5},{3,7},... | collective-permute-start | bytes 196616 | tf_op jit(solution)/shard_map/ppermute | solution.py:351
  40.1 1.4 %collective-permute-start.12 = (bf16[128,256]{1,0:T(8,128)(2,1)S(1)}, bf16[128,256]{1,0:T(8,128)(2,1)S(1)}, u32[]{:S(2)}, u32[]{:S(2)}) collective-permute-start(bf16[128,256]{1,0:T(8,128)(2,1)S(1)} %get-tuple-element.75), channel_id=1, source_target_pairs={{0,8},{2,10},{4,12},{6,14},{8,0},{10,2},{12,4},{14,6},{1,9},{3,11}... | collective-permute-start | bytes 196616 | tf_op jit(solution)/shard_map/ppermute | solution.py:351
  41.4 1.5 %collective-permute-start.13 = (bf16[128,256]{1,0:T(8,128)(2,1)S(1)}, bf16[128,256]{1,0:T(8,128)(2,1)S(1)}, u32[]{:S(2)}, u32[]{:S(2)}) collective-permute-start(bf16[128,256]{1,0:T(8,128)(2,1)S(1)} %get-tuple-element.76), channel_id=1, source_target_pairs={{0,2},{2,0},{4,6},{6,4},{8,10},{10,8},{12,14},{14,12},{1,3},{3,1},... | collective-permute-start | bytes 196616 | tf_op jit(solution)/shard_map/ppermute | solution.py:351
  42.9 0.8 %shard_map.82 = (f32[512,256]{1,0:T(8,128)}, f32[512,256]{1,0:T(8,128)}) custom-call(f32[512,256]{1,0:T(8,128)S(1)} %get-tuple-element.63.q_ref, f32[512,256]{1,0:T(8,128)S(1)} %get-tuple-element.50.u_ref, f32[1024,256]{1,0:T(8,128)S(1)} %get-tuple-element.47.inverse_ref, f32[8,256]{1,0:T(8,128)S(1)} %get-tuple-element.54.rates_ref, ...), custom_call_target="tpu_custom_call" | custom-call | tf_op jit(solution)/shard_map/pallas_call | solution.py:365
  43.7 0.0 collective-permute-done.9.refs_0_
  43.8 3.1 %collective-permute-done.10.refs_1_ = bf16[128,256]{1,0:T(8,128)(2,1)S(1)} collective-permute-done((bf16[128,256]{1,0:T(8,128)(2,1)S(1)}, bf16[128,256]{1,0:T(8,128)(2,1)S(1)}, u32[]{:S(2)}, u32[]{:S(2)}) %collective-permute-start.10) | collective-permute-done | bytes 65568 | tf_op jit(solution)/shard_map/ppermute | solution.py:351
  46.9 0.0 collective-permute-done.11.refs_2_
  46.9 0.0 collective-permute-done.12.refs_3_
  46.9 1.0 %shard_map.83 = (f32[512,256]{1,0:T(8,128)}, f32[512,256]{1,0:T(8,128)}) custom-call(f32[512,256]{1,0:T(8,128)S(1)} %get-tuple-element.63.q_ref, f32[512,256]{1,0:T(8,128)S(1)} %get-tuple-element.50.u_ref, f32[1024,256]{1,0:T(8,128)S(1)} %get-tuple-element.47.inverse_ref, ...), custom_call_target="tpu_custom_call", output_to_operand_aliasing={{0}: (9, {}), {1}: (10, {})} | custom-call | tf_op jit(solution)/shard_map/pallas_call | solution.py:365
  (7 shorter events, 0.0 us)
Async XLA Ops:
  5.8 2.1 %collective-permute-start = (bf16[1024,256]{1,0:T(8,128)(2,1)S(1)}, bf16[1024,256]{1,0:T(8,128)(2,1)S(1)}, u32[]{:S(2)}, u32[]{:S(2)}) collective-permute-start(bf16[1024,256]{1,0:T(8,128)(2,1)S(1)} %get-tuple-element.45), channel_id=1, source_target_pairs={{0,1},{1,0},{2,3},{3,2},{4,5},{5,4},{6,7},{7,6},{8,9},{9,8},{10,11... | collective-permute-start | bytes 1572872 | tf_op jit(solution)/shard_map/ppermute | solution.py:330
  9.3 2.0 %collective-permute-start.1 = (f32[512,256]{1,0:T(8,128)S(1)}, f32[512,256]{1,0:T(8,128)S(1)}, u32[]{:S(2)}, u32[]{:S(2)}) collective-permute-start(f32[512,256]{1,0:T(8,128)S(1)} %get-tuple-element.53), channel_id=1, source_target_pairs={{0,1},{1,0},{2,3},{3,2},{4,5},{5,4},{6,7},{7,6},{8,9},{9,8},{10,11... | collective-permute-start | bytes 1572872 | tf_op jit(solution)/shard_map/ppermute | solution.py:336
  11.5 8.8 %collective-permute-start.2 = (bf16[264,128]{1,0:T(8,128)(2,1)S(1)}, bf16[264,128]{1,0:T(8,128)(2,1)S(1)}, u32[]{:S(2)}, u32[]{:S(2)}) collective-permute-start(bf16[264,128]{1,0:T(8,128)(2,1)S(1)} %get-tuple-element.65), channel_id=1, source_target_pairs={{0,2},{2,0},{4,6},{6,4},{8,10},{10,8},{12,14},{14,12},{1,3},{3,1},... | collective-permute-start | bytes 202760 | tf_op jit(solution)/shard_map/ppermute | solution.py:351
  14.4 9.5 %collective-permute-start.3 = (bf16[264,128]{1,0:T(8,128)(2,1)S(1)}, bf16[264,128]{1,0:T(8,128)(2,1)S(1)}, u32[]{:S(2)}, u32[]{:S(2)}) collective-permute-start(bf16[264,128]{1,0:T(8,128)(2,1)S(1)} %get-tuple-element.66), channel_id=1, source_target_pairs={{0,4},{2,6},{4,0},{6,2},{8,12},{10,14},{12,8},{14,10},{1,5},{3,7},... | collective-permute-start | bytes 202760 | tf_op jit(solution)/shard_map/ppermute | solution.py:351
  16.0 7.9 %collective-permute-start.4 = (bf16[264,128]{1,0:T(8,128)(2,1)S(1)}, bf16[264,128]{1,0:T(8,128)(2,1)S(1)}, u32[]{:S(2)}, u32[]{:S(2)}) collective-permute-start(bf16[264,128]{1,0:T(8,128)(2,1)S(1)} %get-tuple-element.67), channel_id=1, source_target_pairs={{0,6},{2,4},{4,2},{6,0},{8,14},{10,12},{12,10},{14,8},{1,7},{3,5},... | collective-permute-start | bytes 202760 | tf_op jit(solution)/shard_map/ppermute | solution.py:351
  16.0 7.9 %collective-permute-start.5 = (bf16[264,128]{1,0:T(8,128)(2,1)S(1)}, bf16[264,128]{1,0:T(8,128)(2,1)S(1)}, u32[]{:S(2)}, u32[]{:S(2)}) collective-permute-start(bf16[264,128]{1,0:T(8,128)(2,1)S(1)} %get-tuple-element.68), channel_id=1, source_target_pairs={{0,8},{2,10},{4,12},{6,14},{8,0},{10,2},{12,4},{14,6},{1,9},{3,11}... | collective-permute-start | bytes 202760 | tf_op jit(solution)/shard_map/ppermute | solution.py:351
  19.0 10.7 %collective-permute-start.6 = (bf16[264,128]{1,0:T(8,128)(2,1)S(1)}, bf16[264,128]{1,0:T(8,128)(2,1)S(1)}, u32[]{:S(2)}, u32[]{:S(2)}) collective-permute-start(bf16[264,128]{1,0:T(8,128)(2,1)S(1)} %get-tuple-element.69), channel_id=1, source_target_pairs={{0,10},{2,8},{4,14},{6,12},{8,2},{10,0},{12,6},{14,4},{1,11},{3,9}... | collective-permute-start | bytes 202760 | tf_op jit(solution)/shard_map/ppermute | solution.py:351
  20.3 9.4 %collective-permute-start.7 = (bf16[264,128]{1,0:T(8,128)(2,1)S(1)}, bf16[264,128]{1,0:T(8,128)(2,1)S(1)}, u32[]{:S(2)}, u32[]{:S(2)}) collective-permute-start(bf16[264,128]{1,0:T(8,128)(2,1)S(1)} %get-tuple-element.70), channel_id=1, source_target_pairs={{0,12},{2,14},{4,8},{6,10},{8,4},{10,6},{12,0},{14,2},{1,13},{3,15... | collective-permute-start | bytes 202760 | tf_op jit(solution)/shard_map/ppermute | solution.py:351
  23.9 7.1 %collective-permute-start.8 = (bf16[264,128]{1,0:T(8,128)(2,1)S(1)}, bf16[264,128]{1,0:T(8,128)(2,1)S(1)}, u32[]{:S(2)}, u32[]{:S(2)}) collective-permute-start(bf16[264,128]{1,0:T(8,128)(2,1)S(1)} %get-tuple-element.71), channel_id=1, source_target_pairs={{0,14},{2,12},{4,10},{6,8},{8,6},{10,4},{12,2},{14,0},{1,15},{3,13... | collective-permute-start | bytes 202760 | tf_op jit(solution)/shard_map/ppermute | solution.py:351
  31.7 8.4 %collective-permute-start.14 = (bf16[128,256]{1,0:T(8,128)(2,1)S(1)}, bf16[128,256]{1,0:T(8,128)(2,1)S(1)}, u32[]{:S(2)}, u32[]{:S(2)}) collective-permute-start(bf16[128,256]{1,0:T(8,128)(2,1)S(1)} %get-tuple-element.78), channel_id=1, source_target_pairs={{0,14},{2,12},{4,10},{6,8},{8,6},{10,4},{12,2},{14,0},{1,15},{3,13... | collective-permute-start | bytes 196616 | tf_op jit(solution)/shard_map/ppermute | solution.py:351
  33.6 7.8 %collective-permute-start.15 = (bf16[128,256]{1,0:T(8,128)(2,1)S(1)}, bf16[128,256]{1,0:T(8,128)(2,1)S(1)}, u32[]{:S(2)}, u32[]{:S(2)}) collective-permute-start(bf16[128,256]{1,0:T(8,128)(2,1)S(1)} %get-tuple-element.79), channel_id=1, source_target_pairs={{0,12},{2,14},{4,8},{6,10},{8,4},{10,6},{12,0},{14,2},{1,13},{3,15... | collective-permute-start | bytes 196616 | tf_op jit(solution)/shard_map/ppermute | solution.py:351
  35.5 8.2 %collective-permute-start.9 = (bf16[128,256]{1,0:T(8,128)(2,1)S(1)}, bf16[128,256]{1,0:T(8,128)(2,1)S(1)}, u32[]{:S(2)}, u32[]{:S(2)}) collective-permute-start(bf16[128,256]{1,0:T(8,128)(2,1)S(1)} %get-tuple-element.72), channel_id=1, source_target_pairs={{0,6},{2,4},{4,2},{6,0},{8,14},{10,12},{12,10},{14,8},{1,7},{3,5},... | collective-permute-start | bytes 196616 | tf_op jit(solution)/shard_map/ppermute | solution.py:351
  36.9 9.9 %collective-permute-start.10 = (bf16[128,256]{1,0:T(8,128)(2,1)S(1)}, bf16[128,256]{1,0:T(8,128)(2,1)S(1)}, u32[]{:S(2)}, u32[]{:S(2)}) collective-permute-start(bf16[128,256]{1,0:T(8,128)(2,1)S(1)} %get-tuple-element.73), channel_id=1, source_target_pairs={{0,10},{2,8},{4,14},{6,12},{8,2},{10,0},{12,6},{14,4},{1,11},{3,9}... | collective-permute-start | bytes 196616 | tf_op jit(solution)/shard_map/ppermute | solution.py:351
  38.9 8.0 %collective-permute-start.11 = (bf16[128,256]{1,0:T(8,128)(2,1)S(1)}, bf16[128,256]{1,0:T(8,128)(2,1)S(1)}, u32[]{:S(2)}, u32[]{:S(2)}) collective-permute-start(bf16[128,256]{1,0:T(8,128)(2,1)S(1)} %get-tuple-element.74), channel_id=1, source_target_pairs={{0,4},{2,6},{4,0},{6,2},{8,12},{10,14},{12,8},{14,10},{1,5},{3,7},... | collective-permute-start | bytes 196616 | tf_op jit(solution)/shard_map/ppermute | solution.py:351
  40.1 6.8 %collective-permute-start.12 = (bf16[128,256]{1,0:T(8,128)(2,1)S(1)}, bf16[128,256]{1,0:T(8,128)(2,1)S(1)}, u32[]{:S(2)}, u32[]{:S(2)}) collective-permute-start(bf16[128,256]{1,0:T(8,128)(2,1)S(1)} %get-tuple-element.75), channel_id=1, source_target_pairs={{0,8},{2,10},{4,12},{6,14},{8,0},{10,2},{12,4},{14,6},{1,9},{3,11}... | collective-permute-start | bytes 196616 | tf_op jit(solution)/shard_map/ppermute | solution.py:351
  41.4 5.4 %collective-permute-start.13 = (bf16[128,256]{1,0:T(8,128)(2,1)S(1)}, bf16[128,256]{1,0:T(8,128)(2,1)S(1)}, u32[]{:S(2)}, u32[]{:S(2)}) collective-permute-start(bf16[128,256]{1,0:T(8,128)(2,1)S(1)} %get-tuple-element.76), channel_id=1, source_target_pairs={{0,2},{2,0},{4,6},{6,4},{8,10},{10,8},{12,14},{14,12},{1,3},{3,1},... | collective-permute-start | bytes 196616 | tf_op jit(solution)/shard_map/ppermute | solution.py:351

commit v3 on v2

--- a/solution.py
+++ b/solution.py
@@ -93,7 +93,7 @@
         pieces.append((resid_hbm.at[:, :, cut, :], resid_ref.at[:, :, cut, :]))
     copies = [pltpu.make_async_copy(src, dst, sems.at[k]) for k, (src, dst) in enumerate(pieces)]
     streams = copies[5:]
-    for copy in copies[:4] + streams[:1] + copies[4:5] + streams[1:]:
+    for copy in copies[:3] + streams[:1] + copies[3:5] + streams[1:]:
         copy.start()
 
     for copy in copies[:3]:
@@ -121,7 +121,6 @@
     for k in range(penalty_ref.shape[1]):
         rates = jnp.where(label == k, penalty_ref[0:1, k : k + 1], rates)
     rates_ref[...] = rates
-    inverse_ref[...] = 1.0 / (twice(counts_ref[...]) + rates[0:1])
 
     copies[3].wait()
     rounded = jones_ref[...].astype(jnp.bfloat16)
@@ -131,6 +130,7 @@
         cut = pl.ds(start, size)
         streams[m].wait()
         total = gradient_rows(resid_ref, xs_ref, mask_ref, cut)
+        inverse_ref[cut, :] = 1.0 / (twice(counts_ref[cut, :]) + rates[0:1])
         if m == 0:
             copies[4].wait()
         half, offset = divmod(start, own_rows)
@@ -158,7 +158,7 @@
         start = half_start(1 - lax.axis_index("tm"), own_rows) + m * step
         other_ref[m * step : (m + 1) * step] = gradient_rows(
             resid_ref, xs_ref, mask_ref, pl.ds(pl.multiple_of(start, step), step)
-        )
+        ).astype(WIRE)
 
 
 def own_kernel(
@@ -193,7 +193,7 @@
         rows = pl.ds(offset, block)
         u = u_ref[rows, :]
         inverse = inverse_ref[pl.ds(pl.multiple_of(base + offset, block), block), :]
-        q = (own_ref[rows, :] + theirs_ref[rows, :] - rates * u) * inverse
+        q = (own_ref[rows, :] + theirs_ref[rows, :].astype(F32) - rates * u) * inverse
         q_ref[rows, :] = q
         store_wide(message, block * (u.shape[1] // LANES), block, u + q)
 
@@ -330,7 +330,7 @@
     grad_other = lax.ppermute(sent, "tm", swap)
     u, other, xs = call(
         functools.partial(other_kernel, CHUNKS),
-        [in_vmem((own_rows, cols)), in_vmem((own_rows, cols)), in_vmem((2 * share, rows, cols), bf16)],
+        [in_vmem((own_rows, cols)), in_vmem((own_rows, cols), WIRE), in_vmem((2 * share, rows, cols), bf16)],
         [vmem] * 6, 24,
     )(resid, grad, grad_other, masks, inverse, duals0)
     theirs = lax.ppermute(other, "tm", swap)

time: 48 us -> 47.7 us (level)
  transfers between devices with their start and end apart: 16 -> 16, of which waited for: 5 -> 4; matrix products, arithmetic and copies ran while one was open for 0% -> 0% of each run, Pallas kernels for 4% -> 4%
where the time goes in v3:
time: 47.7 us; the launch traced here: 47.4 us
  starting transfers between devices  24.5 us (51%)
  waiting for transfers between devices  11.7 us (25%)
  Pallas kernels  10.5 us (22%)
  between operations  0.71 us (1%)
    ppermute x14, starting transfers between devices, exchange(): lax.ppermute(parts[s], 'chan', [(f, f ^ s) for f in range(members)])  23.4 us
    ppermute x14, waiting for transfers between devices, exchange(): lax.ppermute(parts[s], 'chan', [(f, f ^ s) for f in range(members)])  10.2 us
    pallas_call x1, Pallas kernels, on_device(): call(first_kernel, [in_vmem(residuals.shape[1:], bf16), in_vmem((rows, co...  5.15 us
    pallas_call x2, Pallas kernels, on_device(): call(functools.partial(finish_kernel, members, group), [shape_of((own_row...  1.78 us
    ppermute x1, waiting for transfers between devices, on_device(): grad_other = lax.ppermute(sent, 'tm', swap)  1.54 us
    pallas_call x1, Pallas kernels, on_device(): call(functools.partial(other_kernel, CHUNKS), [in_vmem((own_rows, cols)),...  1.44 us
    pallas_call x1, Pallas kernels, on_device(): call(functools.partial(own_kernel, CHUNKS, members), [in_vmem((own_rows,...  1.28 us
  transfers between devices with their start and end apart: 16, of which 4 were waited for; matrix products, arithmetic and copies ran while one was open for 0% of the time, Pallas kernels for 4%

profile of v3, /device:TPU:0, one launch (start us, length us, event | category | flops | bytes accessed | tf_op | source)
XLA Modules:
  0.0 47.4 jit_solution(6825951236822094592)
XLA Ops:
  0.6 5.1 %shard_map.77 = (bf16[2,2,1024,1024]{3,2,1,0:T(8,128)(2,1)S(1)}, f32[1024,256]{1,0:T(8,128)S(1)}, bf16[1024,256]{1,0:T(8,128)(2,1)S(1)}, f32[2,1024,128]{2,1,0:T...) custom-call(bf16[2,2,1024,1024]{3,2,1,0:T(8,128)(2,1)} %bitcast.8, ...), custom_call_target="tpu_custom_call" | custom-call | tf_op jit(solution)/shard_map/pallas_call | solution.py:312
  5.8 0.6 %collective-permute-start = (bf16[1024,256]{1,0:T(8,128)(2,1)S(1)}, bf16[1024,256]{1,0:T(8,128)(2,1)S(1)}, u32[]{:S(2)}, u32[]{:S(2)}) collective-permute-start(bf16[1024,256]{1,0:T(8,128)(2,1)S(1)} %get-tuple-element.45), channel_id=1, source_target_pairs={{0,1},{1,0},{2,3},{3,2},{4,5},{5,4},{6,7},{7,6},{8,9},{9,8},{10,11... | collective-permute-start | bytes 1572872 | tf_op jit(solution)/shard_map/ppermute | solution.py:330
  6.4 1.5 %collective-permute-done.theirs_ref = bf16[1024,256]{1,0:T(8,128)(2,1)S(1)} collective-permute-done((bf16[1024,256]{1,0:T(8,128)(2,1)S(1)}, bf16[1024,256]{1,0:T(8,128)(2,1)S(1)}, u32[]{:S(2)}, u32[]{:S(2)}) %collective-permute-start) | collective-permute-done | bytes 524320 | tf_op jit(solution)/shard_map/ppermute | solution.py:330
  7.9 1.4 %shard_map.78 = (f32[512,256]{1,0:T(8,128)S(1)}, bf16[512,256]{1,0:T(8,128)(2,1)S(1)}, bf16[4,1024,256]{2,1,0:T(8,128)(2,1)S(1)}) custom-call(bf16[2,2,1024,1024]{3,2,1,0:T(8,128)(2,1)S(1)} %get-tuple-element.43.resid_ref, f32[1024,256]{1,0:T(8,128)S(1)} %get-tuple-element.44.mine_ref, bf16[1024,256]{1,0:T(8,128)(2,1)S(1)} %collective-permute-done.theirs_ref, ...), custom_call_target="tpu_custom_call" | custom-call | tf_op jit(solution)/shard_map/pallas_call | solution.py:331
  9.4 0.4 collective-permute-start.1
  9.8 1.3 %shard_map.79 = (f32[512,256]{1,0:T(8,128)S(1)}, bf16[264,128]{1,0:T(8,128)(2,1)S(1)}, bf16[264,128]{1,0:T(8,128)(2,1)S(1)}, bf16[264,128]{1,0:T(8,128)(2,1)S(1)...) custom-call(bf16[2,2,1024,1024]{3,2,1,0:T(8,128)(2,1)S(1)} %get-tupl, ...), custom_call_target="tpu_custom_call" | custom-call | tf_op jit(solution)/shard_map/pallas_call | solution.py:338
  11.1 0.2 shard_map.80
  11.3 2.8 %collective-permute-start.2 = (bf16[264,128]{1,0:T(8,128)(2,1)S(1)}, bf16[264,128]{1,0:T(8,128)(2,1)S(1)}, u32[]{:S(2)}, u32[]{:S(2)}) collective-permute-start(bf16[264,128]{1,0:T(8,128)(2,1)S(1)} %get-tuple-element.65), channel_id=1, source_target_pairs={{0,2},{2,0},{4,6},{6,4},{8,10},{10,8},{12,14},{14,12},{1,3},{3,1},... | collective-permute-start | bytes 202760 | tf_op jit(solution)/shard_map/ppermute | solution.py:351
  14.0 1.6 %collective-permute-start.3 = (bf16[264,128]{1,0:T(8,128)(2,1)S(1)}, bf16[264,128]{1,0:T(8,128)(2,1)S(1)}, u32[]{:S(2)}, u32[]{:S(2)}) collective-permute-start(bf16[264,128]{1,0:T(8,128)(2,1)S(1)} %get-tuple-element.66), channel_id=1, source_target_pairs={{0,4},{2,6},{4,0},{6,2},{8,12},{10,14},{12,8},{14,10},{1,5},{3,7},... | collective-permute-start | bytes 202760 | tf_op jit(solution)/shard_map/ppermute | solution.py:351
  15.6 0.0 collective-permute-start.4
  15.6 3.0 %collective-permute-start.5 = (bf16[264,128]{1,0:T(8,128)(2,1)S(1)}, bf16[264,128]{1,0:T(8,128)(2,1)S(1)}, u32[]{:S(2)}, u32[]{:S(2)}) collective-permute-start(bf16[264,128]{1,0:T(8,128)(2,1)S(1)} %get-tuple-element.68), channel_id=1, source_target_pairs={{0,8},{2,10},{4,12},{6,14},{8,0},{10,2},{12,4},{14,6},{1,9},{3,11}... | collective-permute-start | bytes 202760 | tf_op jit(solution)/shard_map/ppermute | solution.py:351
  18.6 1.3 %collective-permute-start.6 = (bf16[264,128]{1,0:T(8,128)(2,1)S(1)}, bf16[264,128]{1,0:T(8,128)(2,1)S(1)}, u32[]{:S(2)}, u32[]{:S(2)}) collective-permute-start(bf16[264,128]{1,0:T(8,128)(2,1)S(1)} %get-tuple-element.69), channel_id=1, source_target_pairs={{0,10},{2,8},{4,14},{6,12},{8,2},{10,0},{12,6},{14,4},{1,11},{3,9}... | collective-permute-start | bytes 202760 | tf_op jit(solution)/shard_map/ppermute | solution.py:351
  19.9 0.0 collective-permute-done.2.refs_1_
  19.9 3.6 %collective-permute-start.7 = (bf16[264,128]{1,0:T(8,128)(2,1)S(1)}, bf16[264,128]{1,0:T(8,128)(2,1)S(1)}, u32[]{:S(2)}, u32[]{:S(2)}) collective-permute-start(bf16[264,128]{1,0:T(8,128)(2,1)S(1)} %get-tuple-element.70), channel_id=1, source_target_pairs={{0,12},{2,14},{4,8},{6,10},{8,4},{10,6},{12,0},{14,2},{1,13},{3,15... | collective-permute-start | bytes 202760 | tf_op jit(solution)/shard_map/ppermute | solution.py:351
  23.5 0.0 collective-permute-start.8
  23.5 0.0 collective-permute-done.4.refs_3_
  23.5 0.0 collective-permute-done.5.refs_4_
  23.5 5.6 %collective-permute-done.6.refs_5_ = bf16[264,128]{1,0:T(8,128)(2,1)S(1)} collective-permute-done((bf16[264,128]{1,0:T(8,128)(2,1)S(1)}, bf16[264,128]{1,0:T(8,128)(2,1)S(1)}, u32[]{:S(2)}, u32[]{:S(2)}) %collective-permute-start.6) | collective-permute-done | bytes 67616 | tf_op jit(solution)/shard_map/ppermute | solution.py:351
  29.1 0.0 collective-permute-done.7.refs_6_
  29.1 1.4 %collective-permute-done.8.refs_7_ = bf16[264,128]{1,0:T(8,128)(2,1)S(1)} collective-permute-done((bf16[264,128]{1,0:T(8,128)(2,1)S(1)}, bf16[264,128]{1,0:T(8,128)(2,1)S(1)}, u32[]{:S(2)}, u32[]{:S(2)}) %collective-permute-start.8) | collective-permute-done | bytes 67616 | tf_op jit(solution)/shard_map/ppermute | solution.py:351
  30.6 0.7 %shard_map.81 = (bf16[128,256]{1,0:T(8,128)(2,1)S(1)}, bf16[128,256]{1,0:T(8,128)(2,1)S(1)}, bf16[128,256]{1,0:T(8,128)(2,1)S(1)}, bf16[128,256]{1,0:T(8,128)(2,...) custom-call(f32[8,256]{1,0:T(8,128)S(1)} %get-tuple-element.54.rates, ...), custom_call_target="tpu_custom_call" | custom-call | tf_op jit(solution)/shard_map/pallas_call | solution.py:355
  31.3 2.1 %collective-permute-start.14 = (bf16[128,256]{1,0:T(8,128)(2,1)S(1)}, bf16[128,256]{1,0:T(8,128)(2,1)S(1)}, u32[]{:S(2)}, u32[]{:S(2)}) collective-permute-start(bf16[128,256]{1,0:T(8,128)(2,1)S(1)} %get-tuple-element.78), channel_id=1, source_target_pairs={{0,14},{2,12},{4,10},{6,8},{8,6},{10,4},{12,2},{14,0},{1,15},{3,13... | collective-permute-start | bytes 196616 | tf_op jit(solution)/shard_map/ppermute | solution.py:351
  33.4 1.7 %collective-permute-start.15 = (bf16[128,256]{1,0:T(8,128)(2,1)S(1)}, bf16[128,256]{1,0:T(8,128)(2,1)S(1)}, u32[]{:S(2)}, u32[]{:S(2)}) collective-permute-start(bf16[128,256]{1,0:T(8,128)(2,1)S(1)} %get-tuple-element.79), channel_id=1, source_target_pairs={{0,12},{2,14},{4,8},{6,10},{8,4},{10,6},{12,0},{14,2},{1,13},{3,15... | collective-permute-start | bytes 196616 | tf_op jit(solution)/shard_map/ppermute | solution.py:351
  35.1 1.4 %collective-permute-start.9 = (bf16[128,256]{1,0:T(8,128)(2,1)S(1)}, bf16[128,256]{1,0:T(8,128)(2,1)S(1)}, u32[]{:S(2)}, u32[]{:S(2)}) collective-permute-start(bf16[128,256]{1,0:T(8,128)(2,1)S(1)} %get-tuple-element.72), channel_id=1, source_target_pairs={{0,6},{2,4},{4,2},{6,0},{8,14},{10,12},{12,10},{14,8},{1,7},{3,5},... | collective-permute-start | bytes 196616 | tf_op jit(solution)/shard_map/ppermute | solution.py:351
  36.6 2.1 %collective-permute-start.10 = (bf16[128,256]{1,0:T(8,128)(2,1)S(1)}, bf16[128,256]{1,0:T(8,128)(2,1)S(1)}, u32[]{:S(2)}, u32[]{:S(2)}) collective-permute-start(bf16[128,256]{1,0:T(8,128)(2,1)S(1)} %get-tuple-element.73), channel_id=1, source_target_pairs={{0,10},{2,8},{4,14},{6,12},{8,2},{10,0},{12,6},{14,4},{1,11},{3,9}... | collective-permute-start | bytes 196616 | tf_op jit(solution)/shard_map/ppermute | solution.py:351
  38.7 1.1 %collective-permute-start.11 = (bf16[128,256]{1,0:T(8,128)(2,1)S(1)}, bf16[128,256]{1,0:T(8,128)(2,1)S(1)}, u32[]{:S(2)}, u32[]{:S(2)}) collective-permute-start(bf16[128,256]{1,0:T(8,128)(2,1)S(1)} %get-tuple-element.74), channel_id=1, source_target_pairs={{0,4},{2,6},{4,0},{6,2},{8,12},{10,14},{12,8},{14,10},{1,5},{3,7},... | collective-permute-start | bytes 196616 | tf_op jit(solution)/shard_map/ppermute | solution.py:351
  39.8 1.8 %collective-permute-start.12 = (bf16[128,256]{1,0:T(8,128)(2,1)S(1)}, bf16[128,256]{1,0:T(8,128)(2,1)S(1)}, u32[]{:S(2)}, u32[]{:S(2)}) collective-permute-start(bf16[128,256]{1,0:T(8,128)(2,1)S(1)} %get-tuple-element.75), channel_id=1, source_target_pairs={{0,8},{2,10},{4,12},{6,14},{8,0},{10,2},{12,4},{14,6},{1,9},{3,11}... | collective-permute-start | bytes 196616 | tf_op jit(solution)/shard_map/ppermute | solution.py:351
  41.6 0.0 collective-permute-done.15.refs_2_
  41.6 0.9 %collective-permute-start.13 = (bf16[128,256]{1,0:T(8,128)(2,1)S(1)}, bf16[128,256]{1,0:T(8,128)(2,1)S(1)}, u32[]{:S(2)}, u32[]{:S(2)}) collective-permute-start(bf16[128,256]{1,0:T(8,128)(2,1)S(1)} %get-tuple-element.76), channel_id=1, source_target_pairs={{0,2},{2,0},{4,6},{6,4},{8,10},{10,8},{12,14},{14,12},{1,3},{3,1},... | collective-permute-start | bytes 196616 | tf_op jit(solution)/shard_map/ppermute | solution.py:351
  42.5 0.8 %shard_map.82 = (f32[512,256]{1,0:T(8,128)}, f32[512,256]{1,0:T(8,128)}) custom-call(f32[512,256]{1,0:T(8,128)S(1)} %get-tuple-element.63.q_ref, f32[512,256]{1,0:T(8,128)S(1)} %get-tuple-element.50.u_ref, f32[1024,256]{1,0:T(8,128)S(1)} %get-tuple-element.47.inverse_ref, f32[8,256]{1,0:T(8,128)S(1)} %get-tuple-element.54.rates_ref, ...), custom_call_target="tpu_custom_call" | custom-call | tf_op jit(solution)/shard_map/pallas_call | solution.py:365
  43.4 3.1 %collective-permute-done.10.refs_1_ = bf16[128,256]{1,0:T(8,128)(2,1)S(1)} collective-permute-done((bf16[128,256]{1,0:T(8,128)(2,1)S(1)}, bf16[128,256]{1,0:T(8,128)(2,1)S(1)}, u32[]{:S(2)}, u32[]{:S(2)}) %collective-permute-start.10) | collective-permute-done | bytes 65568 | tf_op jit(solution)/shard_map/ppermute | solution.py:351
  46.5 1.0 %shard_map.83 = (f32[512,256]{1,0:T(8,128)}, f32[512,256]{1,0:T(8,128)}) custom-call(f32[512,256]{1,0:T(8,128)S(1)} %get-tuple-element.63.q_ref, f32[512,256]{1,0:T(8,128)S(1)} %get-tuple-element.50.u_ref, f32[1024,256]{1,0:T(8,128)S(1)} %get-tuple-element.47.inverse_ref, ...), custom_call_target="tpu_custom_call", output_to_operand_aliasing={{0}: (9, {}), {1}: (10, {})} | custom-call | tf_op jit(solution)/shard_map/pallas_call | solution.py:365
  (7 shorter events, 0.0 us)
Async XLA Ops:
  5.8 2.1 %collective-permute-start = (bf16[1024,256]{1,0:T(8,128)(2,1)S(1)}, bf16[1024,256]{1,0:T(8,128)(2,1)S(1)}, u32[]{:S(2)}, u32[]{:S(2)}) collective-permute-start(bf16[1024,256]{1,0:T(8,128)(2,1)S(1)} %get-tuple-element.45), channel_id=1, source_target_pairs={{0,1},{1,0},{2,3},{3,2},{4,5},{5,4},{6,7},{7,6},{8,9},{9,8},{10,11... | collective-permute-start | bytes 1572872 | tf_op jit(solution)/shard_map/ppermute | solution.py:330
  9.4 1.7 %collective-permute-start.1 = (bf16[512,256]{1,0:T(8,128)(2,1)S(1)}, bf16[512,256]{1,0:T(8,128)(2,1)S(1)}, u32[]{:S(2)}, u32[]{:S(2)}) collective-permute-start(bf16[512,256]{1,0:T(8,128)(2,1)S(1)} %get-tuple-element.53), channel_id=1, source_target_pairs={{0,1},{1,0},{2,3},{3,2},{4,5},{5,4},{6,7},{7,6},{8,9},{9,8},{10,11... | collective-permute-start | bytes 786440 | tf_op jit(solution)/shard_map/ppermute | solution.py:336
  11.3 8.6 %collective-permute-start.2 = (bf16[264,128]{1,0:T(8,128)(2,1)S(1)}, bf16[264,128]{1,0:T(8,128)(2,1)S(1)}, u32[]{:S(2)}, u32[]{:S(2)}) collective-permute-start(bf16[264,128]{1,0:T(8,128)(2,1)S(1)} %get-tuple-element.65), channel_id=1, source_target_pairs={{0,2},{2,0},{4,6},{6,4},{8,10},{10,8},{12,14},{14,12},{1,3},{3,1},... | collective-permute-start | bytes 202760 | tf_op jit(solution)/shard_map/ppermute | solution.py:351
  14.0 9.5 %collective-permute-start.3 = (bf16[264,128]{1,0:T(8,128)(2,1)S(1)}, bf16[264,128]{1,0:T(8,128)(2,1)S(1)}, u32[]{:S(2)}, u32[]{:S(2)}) collective-permute-start(bf16[264,128]{1,0:T(8,128)(2,1)S(1)} %get-tuple-element.66), channel_id=1, source_target_pairs={{0,4},{2,6},{4,0},{6,2},{8,12},{10,14},{12,8},{14,10},{1,5},{3,7},... | collective-permute-start | bytes 202760 | tf_op jit(solution)/shard_map/ppermute | solution.py:351
  15.6 7.9 %collective-permute-start.4 = (bf16[264,128]{1,0:T(8,128)(2,1)S(1)}, bf16[264,128]{1,0:T(8,128)(2,1)S(1)}, u32[]{:S(2)}, u32[]{:S(2)}) collective-permute-start(bf16[264,128]{1,0:T(8,128)(2,1)S(1)} %get-tuple-element.67), channel_id=1, source_target_pairs={{0,6},{2,4},{4,2},{6,0},{8,14},{10,12},{12,10},{14,8},{1,7},{3,5},... | collective-permute-start | bytes 202760 | tf_op jit(solution)/shard_map/ppermute | solution.py:351
  15.6 7.9 %collective-permute-start.5 = (bf16[264,128]{1,0:T(8,128)(2,1)S(1)}, bf16[264,128]{1,0:T(8,128)(2,1)S(1)}, u32[]{:S(2)}, u32[]{:S(2)}) collective-permute-start(bf16[264,128]{1,0:T(8,128)(2,1)S(1)} %get-tuple-element.68), channel_id=1, source_target_pairs={{0,8},{2,10},{4,12},{6,14},{8,0},{10,2},{12,4},{14,6},{1,9},{3,11}... | collective-permute-start | bytes 202760 | tf_op jit(solution)/shard_map/ppermute | solution.py:351
  18.6 10.5 %collective-permute-start.6 = (bf16[264,128]{1,0:T(8,128)(2,1)S(1)}, bf16[264,128]{1,0:T(8,128)(2,1)S(1)}, u32[]{:S(2)}, u32[]{:S(2)}) collective-permute-start(bf16[264,128]{1,0:T(8,128)(2,1)S(1)} %get-tuple-element.69), channel_id=1, source_target_pairs={{0,10},{2,8},{4,14},{6,12},{8,2},{10,0},{12,6},{14,4},{1,11},{3,9}... | collective-permute-start | bytes 202760 | tf_op jit(solution)/shard_map/ppermute | solution.py:351
  19.9 9.2 %collective-permute-start.7 = (bf16[264,128]{1,0:T(8,128)(2,1)S(1)}, bf16[264,128]{1,0:T(8,128)(2,1)S(1)}, u32[]{:S(2)}, u32[]{:S(2)}) collective-permute-start(bf16[264,128]{1,0:T(8,128)(2,1)S(1)} %get-tuple-element.70), channel_id=1, source_target_pairs={{0,12},{2,14},{4,8},{6,10},{8,4},{10,6},{12,0},{14,2},{1,13},{3,15... | collective-permute-start | bytes 202760 | tf_op jit(solution)/shard_map/ppermute | solution.py:351
  23.5 7.1 %collective-permute-start.8 = (bf16[264,128]{1,0:T(8,128)(2,1)S(1)}, bf16[264,128]{1,0:T(8,128)(2,1)S(1)}, u32[]{:S(2)}, u32[]{:S(2)}) collective-permute-start(bf16[264,128]{1,0:T(8,128)(2,1)S(1)} %get-tuple-element.71), channel_id=1, source_target_pairs={{0,14},{2,12},{4,10},{6,8},{8,6},{10,4},{12,2},{14,0},{1,15},{3,13... | collective-permute-start | bytes 202760 | tf_op jit(solution)/shard_map/ppermute | solution.py:351
  31.3 8.5 %collective-permute-start.14 = (bf16[128,256]{1,0:T(8,128)(2,1)S(1)}, bf16[128,256]{1,0:T(8,128)(2,1)S(1)}, u32[]{:S(2)}, u32[]{:S(2)}) collective-permute-start(bf16[128,256]{1,0:T(8,128)(2,1)S(1)} %get-tuple-element.78), channel_id=1, source_target_pairs={{0,14},{2,12},{4,10},{6,8},{8,6},{10,4},{12,2},{14,0},{1,15},{3,13... | collective-permute-start | bytes 196616 | tf_op jit(solution)/shard_map/ppermute | solution.py:351
  33.4 8.2 %collective-permute-start.15 = (bf16[128,256]{1,0:T(8,128)(2,1)S(1)}, bf16[128,256]{1,0:T(8,128)(2,1)S(1)}, u32[]{:S(2)}, u32[]{:S(2)}) collective-permute-start(bf16[128,256]{1,0:T(8,128)(2,1)S(1)} %get-tuple-element.79), channel_id=1, source_target_pairs={{0,12},{2,14},{4,8},{6,10},{8,4},{10,6},{12,0},{14,2},{1,13},{3,15... | collective-permute-start | bytes 196616 | tf_op jit(solution)/shard_map/ppermute | solution.py:351
  35.1 8.2 %collective-permute-start.9 = (bf16[128,256]{1,0:T(8,128)(2,1)S(1)}, bf16[128,256]{1,0:T(8,128)(2,1)S(1)}, u32[]{:S(2)}, u32[]{:S(2)}) collective-permute-start(bf16[128,256]{1,0:T(8,128)(2,1)S(1)} %get-tuple-element.72), channel_id=1, source_target_pairs={{0,6},{2,4},{4,2},{6,0},{8,14},{10,12},{12,10},{14,8},{1,7},{3,5},... | collective-permute-start | bytes 196616 | tf_op jit(solution)/shard_map/ppermute | solution.py:351
  36.6 9.9 %collective-permute-start.10 = (bf16[128,256]{1,0:T(8,128)(2,1)S(1)}, bf16[128,256]{1,0:T(8,128)(2,1)S(1)}, u32[]{:S(2)}, u32[]{:S(2)}) collective-permute-start(bf16[128,256]{1,0:T(8,128)(2,1)S(1)} %get-tuple-element.73), channel_id=1, source_target_pairs={{0,10},{2,8},{4,14},{6,12},{8,2},{10,0},{12,6},{14,4},{1,11},{3,9}... | collective-permute-start | bytes 196616 | tf_op jit(solution)/shard_map/ppermute | solution.py:351
  38.7 7.8 %collective-permute-start.11 = (bf16[128,256]{1,0:T(8,128)(2,1)S(1)}, bf16[128,256]{1,0:T(8,128)(2,1)S(1)}, u32[]{:S(2)}, u32[]{:S(2)}) collective-permute-start(bf16[128,256]{1,0:T(8,128)(2,1)S(1)} %get-tuple-element.74), channel_id=1, source_target_pairs={{0,4},{2,6},{4,0},{6,2},{8,12},{10,14},{12,8},{14,10},{1,5},{3,7},... | collective-permute-start | bytes 196616 | tf_op jit(solution)/shard_map/ppermute | solution.py:351
  39.8 6.7 %collective-permute-start.12 = (bf16[128,256]{1,0:T(8,128)(2,1)S(1)}, bf16[128,256]{1,0:T(8,128)(2,1)S(1)}, u32[]{:S(2)}, u32[]{:S(2)}) collective-permute-start(bf16[128,256]{1,0:T(8,128)(2,1)S(1)} %get-tuple-element.75), channel_id=1, source_target_pairs={{0,8},{2,10},{4,12},{6,14},{8,0},{10,2},{12,4},{14,6},{1,9},{3,11}... | collective-permute-start | bytes 196616 | tf_op jit(solution)/shard_map/ppermute | solution.py:351
  41.6 4.9 %collective-permute-start.13 = (bf16[128,256]{1,0:T(8,128)(2,1)S(1)}, bf16[128,256]{1,0:T(8,128)(2,1)S(1)}, u32[]{:S(2)}, u32[]{:S(2)}) collective-permute-start(bf16[128,256]{1,0:T(8,128)(2,1)S(1)} %get-tuple-element.76), channel_id=1, source_target_pairs={{0,2},{2,0},{4,6},{6,4},{8,10},{10,8},{12,14},{14,12},{1,3},{3,1},... | collective-permute-start | bytes 196616 | tf_op jit(solution)/shard_map/ppermute | solution.py:351

commit v4 on v3

--- a/solution.py
+++ b/solution.py
@@ -93,7 +93,7 @@
         pieces.append((resid_hbm.at[:, :, cut, :], resid_ref.at[:, :, cut, :]))
     copies = [pltpu.make_async_copy(src, dst, sems.at[k]) for k, (src, dst) in enumerate(pieces)]
     streams = copies[5:]
-    for copy in copies[:3] + streams[:1] + copies[3:5] + streams[1:]:
+    for copy in copies[:4] + streams[:1] + copies[4:5] + streams[1:]:
         copy.start()
 
     for copy in copies[:3]:
@@ -121,6 +121,7 @@
     for k in range(penalty_ref.shape[1]):
         rates = jnp.where(label == k, penalty_ref[0:1, k : k + 1], rates)
     rates_ref[...] = rates
+    inverse_ref[...] = 1.0 / (twice(counts_ref[...]) + rates[0:1])
 
     copies[3].wait()
     rounded = jones_ref[...].astype(jnp.bfloat16)
@@ -130,7 +131,6 @@
         cut = pl.ds(start, size)
         streams[m].wait()
         total = gradient_rows(resid_ref, xs_ref, mask_ref, cut)
-        inverse_ref[cut, :] = 1.0 / (twice(counts_ref[cut, :]) + rates[0:1])
         if m == 0:
             copies[4].wait()
         half, offset = divmod(start, own_rows)
@@ -291,7 +291,7 @@
 PIECES = 8
 PARTS = (2, 2, 2, 2)
 CHUNKS = 1
-EARLY = 3
+EARLY = 5
 
 
 def partner_order(members):

time: 47.7 us -> 48.7 us (1.021)
  waiting for transfers between devices: 11.7 us -> 12.8 us
    ppermute x14, waiting for transfers between devices: 10.2 us -> 11.2 us  [exchange(): lax.ppermute(parts[s], 'chan', [(f, f ^ s) for f in range(members)])]
  transfers between devices with their start and end apart: 16 -> 16, of which waited for: 4 -> 4; matrix products, arithmetic and copies ran while one was open for 0% -> 0% of each run, Pallas kernels for 4% -> 5%
where the time goes in v4:
time: 48.7 us; the launch traced here: 48.5 us
  starting transfers between devices  24.4 us (50%)
  waiting for transfers between devices  12.8 us (26%)
  Pallas kernels  10.5 us (22%)
  between operations  0.73 us (1%)
    ppermute x14, starting transfers between devices, exchange(): lax.ppermute(parts[s], 'chan', [(f, f ^ s) for f in range(members)])  23.5 us
    ppermute x14, waiting for transfers between devices, exchange(): lax.ppermute(parts[s], 'chan', [(f, f ^ s) for f in range(members)])  11.2 us
    pallas_call x1, Pallas kernels, on_device(): call(first_kernel, [in_vmem(residuals.shape[1:], bf16), in_vmem((rows, co...  5.15 us
    pallas_call x2, Pallas kernels, on_device(): call(functools.partial(finish_kernel, members, group), [shape_of((own_row...  1.78 us
    ppermute x1, waiting for transfers between devices, on_device(): grad_other = lax.ppermute(sent, 'tm', swap)  1.54 us
    pallas_call x1, Pallas kernels, on_device(): call(functools.partial(other_kernel, CHUNKS), [in_vmem((own_rows, cols)),...  1.44 us
    pallas_call x1, Pallas kernels, on_device(): call(functools.partial(own_kernel, CHUNKS, members), [in_vmem((own_rows,...  1.28 us
  transfers between devices with their start and end apart: 16, of which 4 were waited for; matrix products, arithmetic and copies ran while one was open for 0% of the time, Pallas kernels for 5%

profile of v4, /device:TPU:0, one launch (start us, length us, event | category | flops | bytes accessed | tf_op | source)
XLA Modules:
  0.0 48.5 jit_solution(10075986477611348352)
XLA Ops:
  0.6 5.2 %shard_map.77 = (bf16[2,2,1024,1024]{3,2,1,0:T(8,128)(2,1)S(1)}, f32[1024,256]{1,0:T(8,128)S(1)}, bf16[1024,256]{1,0:T(8,128)(2,1)S(1)}, f32[2,1024,128]{2,1,0:T...) custom-call(bf16[2,2,1024,1024]{3,2,1,0:T(8,128)(2,1)} %bitcast.8, ...), custom_call_target="tpu_custom_call" | custom-call | tf_op jit(solution)/shard_map/pallas_call | solution.py:312
  5.8 0.5 %collective-permute-start = (bf16[1024,256]{1,0:T(8,128)(2,1)S(1)}, bf16[1024,256]{1,0:T(8,128)(2,1)S(1)}, u32[]{:S(2)}, u32[]{:S(2)}) collective-permute-start(bf16[1024,256]{1,0:T(8,128)(2,1)S(1)} %get-tuple-element.45), channel_id=1, source_target_pairs={{0,1},{1,0},{2,3},{3,2},{4,5},{5,4},{6,7},{7,6},{8,9},{9,8},{10,11... | collective-permute-start | bytes 1572872 | tf_op jit(solution)/shard_map/ppermute | solution.py:330
  6.3 1.5 %collective-permute-done.theirs_ref = bf16[1024,256]{1,0:T(8,128)(2,1)S(1)} collective-permute-done((bf16[1024,256]{1,0:T(8,128)(2,1)S(1)}, bf16[1024,256]{1,0:T(8,128)(2,1)S(1)}, u32[]{:S(2)}, u32[]{:S(2)}) %collective-permute-start) | collective-permute-done | bytes 524320 | tf_op jit(solution)/shard_map/ppermute | solution.py:330
  7.9 1.4 %shard_map.78 = (f32[512,256]{1,0:T(8,128)S(1)}, bf16[512,256]{1,0:T(8,128)(2,1)S(1)}, bf16[4,1024,256]{2,1,0:T(8,128)(2,1)S(1)}) custom-call(bf16[2,2,1024,1024]{3,2,1,0:T(8,128)(2,1)S(1)} %get-tuple-element.43.resid_ref, f32[1024,256]{1,0:T(8,128)S(1)} %get-tuple-element.44.mine_ref, bf16[1024,256]{1,0:T(8,128)(2,1)S(1)} %collective-permute-done.theirs_ref, ...), custom_call_target="tpu_custom_call" | custom-call | tf_op jit(solution)/shard_map/pallas_call | solution.py:331
  9.3 0.4 collective-permute-start.1
  9.8 1.3 %shard_map.79 = (f32[512,256]{1,0:T(8,128)S(1)}, bf16[264,128]{1,0:T(8,128)(2,1)S(1)}, bf16[264,128]{1,0:T(8,128)(2,1)S(1)}, bf16[264,128]{1,0:T(8,128)(2,1)S(1)...) custom-call(bf16[2,2,1024,1024]{3,2,1,0:T(8,128)(2,1)S(1)} %get-tupl, ...), custom_call_target="tpu_custom_call" | custom-call | tf_op jit(solution)/shard_map/pallas_call | solution.py:338
  11.0 0.0 collective-permute-done.1.theirs_ref
  11.1 0.2 shard_map.80
  11.2 2.8 %collective-permute-start.2 = (bf16[264,128]{1,0:T(8,128)(2,1)S(1)}, bf16[264,128]{1,0:T(8,128)(2,1)S(1)}, u32[]{:S(2)}, u32[]{:S(2)}) collective-permute-start(bf16[264,128]{1,0:T(8,128)(2,1)S(1)} %get-tuple-element.65), channel_id=1, source_target_pairs={{0,2},{2,0},{4,6},{6,4},{8,10},{10,8},{12,14},{14,12},{1,3},{3,1},... | collective-permute-start | bytes 202760 | tf_op jit(solution)/shard_map/ppermute | solution.py:351
  14.0 1.6 %collective-permute-start.3 = (bf16[264,128]{1,0:T(8,128)(2,1)S(1)}, bf16[264,128]{1,0:T(8,128)(2,1)S(1)}, u32[]{:S(2)}, u32[]{:S(2)}) collective-permute-start(bf16[264,128]{1,0:T(8,128)(2,1)S(1)} %get-tuple-element.66), channel_id=1, source_target_pairs={{0,4},{2,6},{4,0},{6,2},{8,12},{10,14},{12,8},{14,10},{1,5},{3,7},... | collective-permute-start | bytes 202760 | tf_op jit(solution)/shard_map/ppermute | solution.py:351
  15.6 0.0 collective-permute-start.4
  15.6 3.0 %collective-permute-start.5 = (bf16[264,128]{1,0:T(8,128)(2,1)S(1)}, bf16[264,128]{1,0:T(8,128)(2,1)S(1)}, u32[]{:S(2)}, u32[]{:S(2)}) collective-permute-start(bf16[264,128]{1,0:T(8,128)(2,1)S(1)} %get-tuple-element.68), channel_id=1, source_target_pairs={{0,8},{2,10},{4,12},{6,14},{8,0},{10,2},{12,4},{14,6},{1,9},{3,11}... | collective-permute-start | bytes 202760 | tf_op jit(solution)/shard_map/ppermute | solution.py:351
  18.6 1.3 %collective-permute-start.6 = (bf16[264,128]{1,0:T(8,128)(2,1)S(1)}, bf16[264,128]{1,0:T(8,128)(2,1)S(1)}, u32[]{:S(2)}, u32[]{:S(2)}) collective-permute-start(bf16[264,128]{1,0:T(8,128)(2,1)S(1)} %get-tuple-element.69), channel_id=1, source_target_pairs={{0,10},{2,8},{4,14},{6,12},{8,2},{10,0},{12,6},{14,4},{1,11},{3,9}... | collective-permute-start | bytes 202760 | tf_op jit(solution)/shard_map/ppermute | solution.py:351
  19.9 0.0 collective-permute-done.2.refs_1_
  19.9 3.6 %collective-permute-start.7 = (bf16[264,128]{1,0:T(8,128)(2,1)S(1)}, bf16[264,128]{1,0:T(8,128)(2,1)S(1)}, u32[]{:S(2)}, u32[]{:S(2)}) collective-permute-start(bf16[264,128]{1,0:T(8,128)(2,1)S(1)} %get-tuple-element.70), channel_id=1, source_target_pairs={{0,12},{2,14},{4,8},{6,10},{8,4},{10,6},{12,0},{14,2},{1,13},{3,15... | collective-permute-start | bytes 202760 | tf_op jit(solution)/shard_map/ppermute | solution.py:351
  23.5 0.0 collective-permute-done.3.refs_2_
  23.5 0.0 collective-permute-done.5.refs_4_
  23.5 5.6 %collective-permute-done.6.refs_5_ = bf16[264,128]{1,0:T(8,128)(2,1)S(1)} collective-permute-done((bf16[264,128]{1,0:T(8,128)(2,1)S(1)}, bf16[264,128]{1,0:T(8,128)(2,1)S(1)}, u32[]{:S(2)}, u32[]{:S(2)}) %collective-permute-start.6) | collective-permute-done | bytes 67616 | tf_op jit(solution)/shard_map/ppermute | solution.py:351
  29.1 0.0 collective-permute-done.7.refs_6_
  29.1 1.5 %collective-permute-done.8.refs_7_ = bf16[264,128]{1,0:T(8,128)(2,1)S(1)} collective-permute-done((bf16[264,128]{1,0:T(8,128)(2,1)S(1)}, bf16[264,128]{1,0:T(8,128)(2,1)S(1)}, u32[]{:S(2)}, u32[]{:S(2)}) %collective-permute-start.8) | collective-permute-done | bytes 67616 | tf_op jit(solution)/shard_map/ppermute | solution.py:351
  30.6 0.7 %shard_map.81 = (bf16[128,256]{1,0:T(8,128)(2,1)S(1)}, bf16[128,256]{1,0:T(8,128)(2,1)S(1)}, bf16[128,256]{1,0:T(8,128)(2,1)S(1)}, bf16[128,256]{1,0:T(8,128)(2,...) custom-call(f32[8,256]{1,0:T(8,128)S(1)} %get-tuple-element.54.rates, ...), custom_call_target="tpu_custom_call" | custom-call | tf_op jit(solution)/shard_map/pallas_call | solution.py:355
  31.3 2.1 %collective-permute-start.12 = (bf16[128,256]{1,0:T(8,128)(2,1)S(1)}, bf16[128,256]{1,0:T(8,128)(2,1)S(1)}, u32[]{:S(2)}, u32[]{:S(2)}) collective-permute-start(bf16[128,256]{1,0:T(8,128)(2,1)S(1)} %get-tuple-element.76), channel_id=1, source_target_pairs={{0,14},{2,12},{4,10},{6,8},{8,6},{10,4},{12,2},{14,0},{1,15},{3,13... | collective-permute-start | bytes 196616 | tf_op jit(solution)/shard_map/ppermute | solution.py:351
  33.4 1.7 %collective-permute-start.13 = (bf16[128,256]{1,0:T(8,128)(2,1)S(1)}, bf16[128,256]{1,0:T(8,128)(2,1)S(1)}, u32[]{:S(2)}, u32[]{:S(2)}) collective-permute-start(bf16[128,256]{1,0:T(8,128)(2,1)S(1)} %get-tuple-element.77), channel_id=1, source_target_pairs={{0,12},{2,14},{4,8},{6,10},{8,4},{10,6},{12,0},{14,2},{1,13},{3,15... | collective-permute-start | bytes 196616 | tf_op jit(solution)/shard_map/ppermute | solution.py:351
  35.1 0.9 %collective-permute-start.9 = (bf16[128,256]{1,0:T(8,128)(2,1)S(1)}, bf16[128,256]{1,0:T(8,128)(2,1)S(1)}, u32[]{:S(2)}, u32[]{:S(2)}) collective-permute-start(bf16[128,256]{1,0:T(8,128)(2,1)S(1)} %get-tuple-element.72), channel_id=1, source_target_pairs={{0,4},{2,6},{4,0},{6,2},{8,12},{10,14},{12,8},{14,10},{1,5},{3,7},... | collective-permute-start | bytes 196616 | tf_op jit(solution)/shard_map/ppermute | solution.py:351
  36.0 2.1 %collective-permute-start.14 = (bf16[128,256]{1,0:T(8,128)(2,1)S(1)}, bf16[128,256]{1,0:T(8,128)(2,1)S(1)}, u32[]{:S(2)}, u32[]{:S(2)}) collective-permute-start(bf16[128,256]{1,0:T(8,128)(2,1)S(1)} %get-tuple-element.78), channel_id=1, source_target_pairs={{0,6},{2,4},{4,2},{6,0},{8,14},{10,12},{12,10},{14,8},{1,7},{3,5},... | collective-permute-start | bytes 196616 | tf_op jit(solution)/shard_map/ppermute | solution.py:351
  38.1 1.7 %collective-permute-start.15 = (bf16[128,256]{1,0:T(8,128)(2,1)S(1)}, bf16[128,256]{1,0:T(8,128)(2,1)S(1)}, u32[]{:S(2)}, u32[]{:S(2)}) collective-permute-start(bf16[128,256]{1,0:T(8,128)(2,1)S(1)} %get-tuple-element.79), channel_id=1, source_target_pairs={{0,10},{2,8},{4,14},{6,12},{8,2},{10,0},{12,6},{14,4},{1,11},{3,9}... | collective-permute-start | bytes 196616 | tf_op jit(solution)/shard_map/ppermute | solution.py:351
  39.8 1.4 %collective-permute-start.10 = (bf16[128,256]{1,0:T(8,128)(2,1)S(1)}, bf16[128,256]{1,0:T(8,128)(2,1)S(1)}, u32[]{:S(2)}, u32[]{:S(2)}) collective-permute-start(bf16[128,256]{1,0:T(8,128)(2,1)S(1)} %get-tuple-element.73), channel_id=1, source_target_pairs={{0,8},{2,10},{4,12},{6,14},{8,0},{10,2},{12,4},{14,6},{1,9},{3,11}... | collective-permute-start | bytes 196616 | tf_op jit(solution)/shard_map/ppermute | solution.py:351
  41.2 1.3 %collective-permute-start.11 = (bf16[128,256]{1,0:T(8,128)(2,1)S(1)}, bf16[128,256]{1,0:T(8,128)(2,1)S(1)}, u32[]{:S(2)}, u32[]{:S(2)}) collective-permute-start(bf16[128,256]{1,0:T(8,128)(2,1)S(1)} %get-tuple-element.74), channel_id=1, source_target_pairs={{0,2},{2,0},{4,6},{6,4},{8,10},{10,8},{12,14},{14,12},{1,3},{3,1},... | collective-permute-start | bytes 196616 | tf_op jit(solution)/shard_map/ppermute | solution.py:351
  42.5 4.1 %collective-permute-done.15.refs_4_ = bf16[128,256]{1,0:T(8,128)(2,1)S(1)} collective-permute-done((bf16[128,256]{1,0:T(8,128)(2,1)S(1)}, bf16[128,256]{1,0:T(8,128)(2,1)S(1)}, u32[]{:S(2)}, u32[]{:S(2)}) %collective-permute-start.15) | collective-permute-done | bytes 65568 | tf_op jit(solution)/shard_map/ppermute | solution.py:351
  46.7 0.9 %shard_map.82 = (f32[512,256]{1,0:T(8,128)}, f32[512,256]{1,0:T(8,128)}) custom-call(f32[512,256]{1,0:T(8,128)S(1)} %get-tuple-element.63.q_ref, f32[512,256]{1,0:T(8,128)S(1)} %get-tuple-element.50.u_ref, f32[1024,256]{1,0:T(8,128)S(1)} %get-tuple-element.47.inverse_ref, f32[8,256]{1,0:T(8,128)S(1)} %get-tuple-element.54.rates_ref, ...), custom_call_target="tpu_custom_call" | custom-call | tf_op jit(solution)/shard_map/pallas_call | solution.py:365
  47.6 0.0 collective-permute-done.11.refs_2_
  47.6 0.8 %shard_map.83 = (f32[512,256]{1,0:T(8,128)}, f32[512,256]{1,0:T(8,128)}) custom-call(f32[512,256]{1,0:T(8,128)S(1)} %get-tuple-element.63.q_ref, f32[512,256]{1,0:T(8,128)S(1)} %get-tuple-element.50.u_ref, f32[1024,256]{1,0:T(8,128)S(1)} %get-tuple-element.47.inverse_ref, ...), custom_call_target="tpu_custom_call", output_to_operand_aliasing={{0}: (7, {}), {1}: (8, {})} | custom-call | tf_op jit(solution)/shard_map/pallas_call | solution.py:365
  (7 shorter events, 0.0 us)
Async XLA Ops:
  5.8 2.1 %collective-permute-start = (bf16[1024,256]{1,0:T(8,128)(2,1)S(1)}, bf16[1024,256]{1,0:T(8,128)(2,1)S(1)}, u32[]{:S(2)}, u32[]{:S(2)}) collective-permute-start(bf16[1024,256]{1,0:T(8,128)(2,1)S(1)} %get-tuple-element.45), channel_id=1, source_target_pairs={{0,1},{1,0},{2,3},{3,2},{4,5},{5,4},{6,7},{7,6},{8,9},{9,8},{10,11... | collective-permute-start | bytes 1572872 | tf_op jit(solution)/shard_map/ppermute | solution.py:330
  9.3 1.7 %collective-permute-start.1 = (bf16[512,256]{1,0:T(8,128)(2,1)S(1)}, bf16[512,256]{1,0:T(8,128)(2,1)S(1)}, u32[]{:S(2)}, u32[]{:S(2)}) collective-permute-start(bf16[512,256]{1,0:T(8,128)(2,1)S(1)} %get-tuple-element.53), channel_id=1, source_target_pairs={{0,1},{1,0},{2,3},{3,2},{4,5},{5,4},{6,7},{7,6},{8,9},{9,8},{10,11... | collective-permute-start | bytes 786440 | tf_op jit(solution)/shard_map/ppermute | solution.py:336
  11.2 8.6 %collective-permute-start.2 = (bf16[264,128]{1,0:T(8,128)(2,1)S(1)}, bf16[264,128]{1,0:T(8,128)(2,1)S(1)}, u32[]{:S(2)}, u32[]{:S(2)}) collective-permute-start(bf16[264,128]{1,0:T(8,128)(2,1)S(1)} %get-tuple-element.65), channel_id=1, source_target_pairs={{0,2},{2,0},{4,6},{6,4},{8,10},{10,8},{12,14},{14,12},{1,3},{3,1},... | collective-permute-start | bytes 202760 | tf_op jit(solution)/shard_map/ppermute | solution.py:351
  14.0 9.5 %collective-permute-start.3 = (bf16[264,128]{1,0:T(8,128)(2,1)S(1)}, bf16[264,128]{1,0:T(8,128)(2,1)S(1)}, u32[]{:S(2)}, u32[]{:S(2)}) collective-permute-start(bf16[264,128]{1,0:T(8,128)(2,1)S(1)} %get-tuple-element.66), channel_id=1, source_target_pairs={{0,4},{2,6},{4,0},{6,2},{8,12},{10,14},{12,8},{14,10},{1,5},{3,7},... | collective-permute-start | bytes 202760 | tf_op jit(solution)/shard_map/ppermute | solution.py:351
  15.6 7.9 %collective-permute-start.4 = (bf16[264,128]{1,0:T(8,128)(2,1)S(1)}, bf16[264,128]{1,0:T(8,128)(2,1)S(1)}, u32[]{:S(2)}, u32[]{:S(2)}) collective-permute-start(bf16[264,128]{1,0:T(8,128)(2,1)S(1)} %get-tuple-element.67), channel_id=1, source_target_pairs={{0,6},{2,4},{4,2},{6,0},{8,14},{10,12},{12,10},{14,8},{1,7},{3,5},... | collective-permute-start | bytes 202760 | tf_op jit(solution)/shard_map/ppermute | solution.py:351
  15.6 7.9 %collective-permute-start.5 = (bf16[264,128]{1,0:T(8,128)(2,1)S(1)}, bf16[264,128]{1,0:T(8,128)(2,1)S(1)}, u32[]{:S(2)}, u32[]{:S(2)}) collective-permute-start(bf16[264,128]{1,0:T(8,128)(2,1)S(1)} %get-tuple-element.68), channel_id=1, source_target_pairs={{0,8},{2,10},{4,12},{6,14},{8,0},{10,2},{12,4},{14,6},{1,9},{3,11}... | collective-permute-start | bytes 202760 | tf_op jit(solution)/shard_map/ppermute | solution.py:351
  18.6 10.5 %collective-permute-start.6 = (bf16[264,128]{1,0:T(8,128)(2,1)S(1)}, bf16[264,128]{1,0:T(8,128)(2,1)S(1)}, u32[]{:S(2)}, u32[]{:S(2)}) collective-permute-start(bf16[264,128]{1,0:T(8,128)(2,1)S(1)} %get-tuple-element.69), channel_id=1, source_target_pairs={{0,10},{2,8},{4,14},{6,12},{8,2},{10,0},{12,6},{14,4},{1,11},{3,9}... | collective-permute-start | bytes 202760 | tf_op jit(solution)/shard_map/ppermute | solution.py:351
  19.9 9.2 %collective-permute-start.7 = (bf16[264,128]{1,0:T(8,128)(2,1)S(1)}, bf16[264,128]{1,0:T(8,128)(2,1)S(1)}, u32[]{:S(2)}, u32[]{:S(2)}) collective-permute-start(bf16[264,128]{1,0:T(8,128)(2,1)S(1)} %get-tuple-element.70), channel_id=1, source_target_pairs={{0,12},{2,14},{4,8},{6,10},{8,4},{10,6},{12,0},{14,2},{1,13},{3,15... | collective-permute-start | bytes 202760 | tf_op jit(solution)/shard_map/ppermute | solution.py:351
  23.5 7.1 %collective-permute-start.8 = (bf16[264,128]{1,0:T(8,128)(2,1)S(1)}, bf16[264,128]{1,0:T(8,128)(2,1)S(1)}, u32[]{:S(2)}, u32[]{:S(2)}) collective-permute-start(bf16[264,128]{1,0:T(8,128)(2,1)S(1)} %get-tuple-element.71), channel_id=1, source_target_pairs={{0,14},{2,12},{4,10},{6,8},{8,6},{10,4},{12,2},{14,0},{1,15},{3,13... | collective-permute-start | bytes 202760 | tf_op jit(solution)/shard_map/ppermute | solution.py:351
  31.3 8.5 %collective-permute-start.12 = (bf16[128,256]{1,0:T(8,128)(2,1)S(1)}, bf16[128,256]{1,0:T(8,128)(2,1)S(1)}, u32[]{:S(2)}, u32[]{:S(2)}) collective-permute-start(bf16[128,256]{1,0:T(8,128)(2,1)S(1)} %get-tuple-element.76), channel_id=1, source_target_pairs={{0,14},{2,12},{4,10},{6,8},{8,6},{10,4},{12,2},{14,0},{1,15},{3,13... | collective-permute-start | bytes 196616 | tf_op jit(solution)/shard_map/ppermute | solution.py:351
  33.4 7.8 %collective-permute-start.13 = (bf16[128,256]{1,0:T(8,128)(2,1)S(1)}, bf16[128,256]{1,0:T(8,128)(2,1)S(1)}, u32[]{:S(2)}, u32[]{:S(2)}) collective-permute-start(bf16[128,256]{1,0:T(8,128)(2,1)S(1)} %get-tuple-element.77), channel_id=1, source_target_pairs={{0,12},{2,14},{4,8},{6,10},{8,4},{10,6},{12,0},{14,2},{1,13},{3,15... | collective-permute-start | bytes 196616 | tf_op jit(solution)/shard_map/ppermute | solution.py:351
  35.1 12.5 %collective-permute-start.9 = (bf16[128,256]{1,0:T(8,128)(2,1)S(1)}, bf16[128,256]{1,0:T(8,128)(2,1)S(1)}, u32[]{:S(2)}, u32[]{:S(2)}) collective-permute-start(bf16[128,256]{1,0:T(8,128)(2,1)S(1)} %get-tuple-element.72), channel_id=1, source_target_pairs={{0,4},{2,6},{4,0},{6,2},{8,12},{10,14},{12,8},{14,10},{1,5},{3,7},... | collective-permute-start | bytes 196616 | tf_op jit(solution)/shard_map/ppermute | solution.py:351
  36.0 6.5 %collective-permute-start.14 = (bf16[128,256]{1,0:T(8,128)(2,1)S(1)}, bf16[128,256]{1,0:T(8,128)(2,1)S(1)}, u32[]{:S(2)}, u32[]{:S(2)}) collective-permute-start(bf16[128,256]{1,0:T(8,128)(2,1)S(1)} %get-tuple-element.78), channel_id=1, source_target_pairs={{0,6},{2,4},{4,2},{6,0},{8,14},{10,12},{12,10},{14,8},{1,7},{3,5},... | collective-permute-start | bytes 196616 | tf_op jit(solution)/shard_map/ppermute | solution.py:351
  38.1 8.5 %collective-permute-start.15 = (bf16[128,256]{1,0:T(8,128)(2,1)S(1)}, bf16[128,256]{1,0:T(8,128)(2,1)S(1)}, u32[]{:S(2)}, u32[]{:S(2)}) collective-permute-start(bf16[128,256]{1,0:T(8,128)(2,1)S(1)} %get-tuple-element.79), channel_id=1, source_target_pairs={{0,10},{2,8},{4,14},{6,12},{8,2},{10,0},{12,6},{14,4},{1,11},{3,9}... | collective-permute-start | bytes 196616 | tf_op jit(solution)/shard_map/ppermute | solution.py:351
  39.8 7.8 %collective-permute-start.10 = (bf16[128,256]{1,0:T(8,128)(2,1)S(1)}, bf16[128,256]{1,0:T(8,128)(2,1)S(1)}, u32[]{:S(2)}, u32[]{:S(2)}) collective-permute-start(bf16[128,256]{1,0:T(8,128)(2,1)S(1)} %get-tuple-element.73), channel_id=1, source_target_pairs={{0,8},{2,10},{4,12},{6,14},{8,0},{10,2},{12,4},{14,6},{1,9},{3,11}... | collective-permute-start | bytes 196616 | tf_op jit(solution)/shard_map/ppermute | solution.py:351
  41.2 6.4 %collective-permute-start.11 = (bf16[128,256]{1,0:T(8,128)(2,1)S(1)}, bf16[128,256]{1,0:T(8,128)(2,1)S(1)}, u32[]{:S(2)}, u32[]{:S(2)}) collective-permute-start(bf16[128,256]{1,0:T(8,128)(2,1)S(1)} %get-tuple-element.74), channel_id=1, source_target_pairs={{0,2},{2,0},{4,6},{6,4},{8,10},{10,8},{12,14},{14,12},{1,3},{3,1},... | collective-permute-start | bytes 196616 | tf_op jit(solution)/shard_map/ppermute | solution.py:351
